TPU v7x, 128 devices: a whole 4x4x4 slice. The times are simulated.
128 devices in a mesh: grp: 8 (over x, core), row: 16 (over z, y).
Axes of the slice: x: 4, y: 4, z: 4, core: 2. Of those that a mesh axis runs over, the one named last changes fastest.
Arguments:
- pair_feats: bfloat16 [32, 6, 128, 128, 128], P('grp', None, 'row'), may hold values from -6 to 6
- block_cols: int32 [32, 6], replicated, may hold values from 0 to 31, as said below
- attn_mask: int32 [32, 6], replicated, may hold values from 0 to 1, as said below
- chain_of_row: int32 [32], replicated, may hold values from 0 to 3
- same_chain: float32 [16], replicated, may hold values from -2 to 2
- node_feats: bfloat16 [4096, 768], P('grp'), may hold values from -6 to 6
- node_cotangent: bfloat16 [4096, 768], P('grp'), may hold values from -6 to 6
- tri_weight: bfloat16 [128, 256], replicated, may hold values from -0.5 to 0.5
- gate_weight: bfloat16 [128, 128], replicated, may hold values from -0.5 to 0.5
- tri_out_weight: bfloat16 [64, 128], replicated, may hold values from -0.75 to 0.75
- bias_weight: bfloat16 [128, 16], replicated, may hold values from -0.5 to 0.5
- query_weight: bfloat16 [768, 768], P(None, 'row'), may hold values from -8 to 8
- key_weight: bfloat16 [768, 768], P(None, 'row'), may hold values from -8 to 8
- value_weight: bfloat16 [768, 768], P(None, 'row'), may hold values from -0.21875 to 0.21875
- out_weight: bfloat16 [768, 768], P('row'), may hold values from -0.21875 to 0.21875
Outputs:
- pair_out: bfloat16 [32, 6, 128, 128, 128], P('grp', None, 'row')
- node_out: bfloat16 [4096, 768], P(('grp', 'row'))
- pair_grad: bfloat16 [32, 6, 128, 128, 128], P('grp', None, 'row')
Inputs may be any that keep to these rules, and one draw needn't show every extreme that they name: `block_cols`: block row I belongs to chain group I // 4. Its 6 columns are distinct: itself in slot 0, the other block rows of its own group, and 2 block rows of other groups. The rows of one group name block rows of at most 4 other groups and at most 2 distinct block rows of any one other group; some pair of groups reaches 2. `attn_mask`: slot 0 of every block row is 1.
All inputs are finite; a program needn't handle non-finite values.
Results may differ from a plain program's by a relative error of at most 0.025.
Values may be sent and summed in bfloat16 or wider, within the bound.
A program may use at most 192 MiB of HBM per device.

v0:
```python
import jax
import jax.numpy as jnp
from jax import lax
from jax.sharding import PartitionSpec as P

CAPX = 2


epsilon = 1e-05


def norm_parts(values, dimension):
    center = jnp.mean(values, axis=dimension, keepdims=True)
    shifted = values - center
    spread = jnp.mean(shifted * shifted, axis=dimension, keepdims=True)
    inverse = lax.rsqrt(spread + epsilon)
    return (shifted * inverse, inverse)


def per_device(
    pair_feats,
    block_cols,
    attn_mask,
    chain_of_row,
    same_chain,
    node_feats,
    node_cotangent,
    tri_weight,
    gate_weight,
    tri_out_weight,
    bias_weight,
    query_weight,
    key_weight,
    value_weight,
    out_weight,
):
    rows_split = lax.axis_size("row")
    group_count = lax.axis_size("grp")
    group_index = lax.axis_index("grp")
    row_index = lax.axis_index("row")
    block_rows = pair_feats.shape[0]
    slot_count = pair_feats.shape[1]
    block_size = pair_feats.shape[3]
    hidden = tri_weight.shape[1] // 4
    hid_part = hidden // rows_split
    head_count = bias_weight.shape[1]
    head_part = head_count // rows_split
    width_part = query_weight.shape[1]
    head_size = width_part // head_part
    total_rows = block_cols.shape[0]
    capacity = CAPX
    first_row = group_index * block_rows
    own_cols = lax.dynamic_slice_in_dim(block_cols, first_row, block_rows, 0)
    pair_float = pair_feats.astype(jnp.float32)
    normed, pair_scale = norm_parts(pair_float, 4)
    normed_short = normed.astype(jnp.bfloat16)
    projected = jnp.einsum(
        "rsijc,cx->rsxij", normed_short, tri_weight, preferred_element_type=jnp.float32
    )
    left_proj = (
        jax.nn.sigmoid(projected[:, :, hidden : 2 * hidden]) * projected[:, :, :hidden]
    ).astype(jnp.bfloat16)
    right_proj = (
        jax.nn.sigmoid(projected[:, :, 3 * hidden :]) * projected[:, :, 2 * hidden : 3 * hidden]
    ).astype(jnp.bfloat16)
    gate_values = jax.nn.sigmoid(
        jnp.einsum("rsijc,cy->rsijy", normed_short, gate_weight, preferred_element_type=jnp.float32)
    ).astype(jnp.bfloat16)
    bias_rows = jnp.einsum(
        "rsijc,ch->rshij", normed_short, bias_weight, preferred_element_type=jnp.float32
    ).astype(jnp.bfloat16)
    left_chan, right_chan, bias_chan = (
        lax.all_to_all(left_proj, "row", split_axis=2, concat_axis=3, tiled=True),
        lax.all_to_all(right_proj, "row", split_axis=2, concat_axis=3, tiled=True),
        lax.all_to_all(bias_rows, "row", split_axis=2, concat_axis=3, tiled=True),
    )
    targets = jnp.arange(total_rows, dtype=jnp.int32)
    group_cols = block_cols.reshape(group_count, block_rows * slot_count)
    named_rows = jnp.max(
        (group_cols[:, :, None] == targets[None, None, :]).astype(jnp.int32), axis=1
    )
    owner_group = targets // block_rows
    outside = (owner_group[None, :] != jnp.arange(group_count, dtype=jnp.int32)[:, None]).astype(
        jnp.int32
    )
    named_rows = named_rows * outside
    named_grouped = named_rows.reshape(group_count, group_count, block_rows)
    slot_rank = (jnp.cumsum(named_grouped, axis=2) - named_grouped).reshape(group_count, total_rows)
    sent_named = lax.dynamic_slice_in_dim(named_rows, first_row, block_rows, 1)
    sent_rank = lax.dynamic_slice_in_dim(slot_rank, first_row, block_rows, 1)
    slot_ids = jnp.arange(capacity, dtype=jnp.int32)
    selection = (
        sent_named[:, None, :]
        * (sent_rank[:, None, :] == slot_ids[None, :, None]).astype(jnp.int32)
    ).astype(jnp.bfloat16)
    my_rank = lax.dynamic_index_in_dim(slot_rank, group_index, 0, keepdims=False)
    outgoing = jnp.einsum(
        "hcl,lsxik->hcsxik", selection, right_proj, preferred_element_type=jnp.float32
    ).astype(jnp.bfloat16)
    arrived = lax.all_to_all(
        lax.all_to_all(outgoing, "grp", split_axis=0, concat_axis=0, tiled=True),
        "row",
        split_axis=3,
        concat_axis=4,
        tiled=True,
    )
    arrived = arrived.reshape(group_count * capacity, slot_count, hid_part, block_size, block_size)
    table = jnp.concatenate([right_chan, arrived], axis=0)
    local_place = jnp.clip(targets - first_row, 0, block_rows - 1)
    remote_place = block_rows + owner_group * capacity + jnp.clip(my_rank, 0, capacity - 1)
    table_place = jnp.where(owner_group == group_index, local_place, remote_place)

    def triangle_row(left_row, row_cols):
        places = jnp.take(table_place, row_cols, axis=0)
        far_rows = jnp.take(table, places, axis=0)
        far_cols = jnp.take(block_cols, row_cols, axis=0)
        matches = (row_cols[None, :, None] == far_cols[:, None, :]).astype(jnp.bfloat16)
        aligned = jnp.einsum(
            "stu,sudjk->stdjk", matches, far_rows, preferred_element_type=jnp.float32
        ).astype(jnp.bfloat16)
        return jnp.einsum(
            "tdik,stdjk->sdij", left_row, aligned, preferred_element_type=jnp.float32
        ).astype(jnp.bfloat16)

    tri_chan = jax.vmap(triangle_row)(left_chan, own_cols)
    node_norm = norm_parts(node_feats.astype(jnp.float32), 1)[0].astype(jnp.bfloat16)
    queries = jnp.dot(node_norm, query_weight, preferred_element_type=jnp.float32).astype(
        jnp.bfloat16
    )
    keys_here = jnp.dot(node_norm, key_weight, preferred_element_type=jnp.float32).astype(
        jnp.bfloat16
    )
    values_here = jnp.dot(node_norm, value_weight, preferred_element_type=jnp.float32).astype(
        jnp.bfloat16
    )
    keys_all, values_all = (
        lax.all_gather(keys_here, "grp", axis=0, tiled=True),
        lax.all_gather(values_here, "grp", axis=0, tiled=True),
    )
    keys_all = keys_all.reshape(total_rows, block_size, head_part, head_size)
    values_all = values_all.reshape(total_rows, block_size, head_part, head_size)
    queries = queries.reshape(block_rows, block_size, head_part, head_size)
    cot_heads = lax.dot_general(
        node_cotangent, out_weight, (((1,), (1,)), ((), ())), preferred_element_type=jnp.float32
    ).astype(jnp.bfloat16)
    cot_heads = cot_heads.reshape(block_rows, block_size, head_part, head_size)
    chain_bias = lax.dynamic_slice_in_dim(same_chain, row_index * head_part, head_part, 0)
    own_chain = lax.dynamic_slice_in_dim(chain_of_row, first_row, block_rows, 0)
    own_mask = lax.dynamic_slice_in_dim(attn_mask, first_row, block_rows, 0)
    score_scale = head_size ** (-0.5)

    def attend_row(query_rows, cot_rows, bias_block, row_cols, row_chain, row_mask):
        near_keys = jnp.take(keys_all, row_cols, axis=0)
        near_values = jnp.take(values_all, row_cols, axis=0)
        same_flag = (jnp.take(chain_of_row, row_cols) == row_chain).astype(jnp.float32)
        scores = (
            jnp.einsum("ihd,sjhd->shij", query_rows, near_keys, preferred_element_type=jnp.float32)
            * score_scale
        )
        scores = (
            scores
            + bias_block.astype(jnp.float32)
            + chain_bias[None, :, None, None] * same_flag[:, None, None, None]
        )
        scores = jnp.where((row_mask > 0)[:, None, None, None], scores, -jnp.inf)
        row_top = jnp.max(scores, axis=(0, 3), keepdims=True)
        exp_scores = jnp.exp(scores - row_top)
        probabilities = exp_scores / jnp.sum(exp_scores, axis=(0, 3), keepdims=True)
        probs_low = probabilities.astype(jnp.bfloat16)
        mixed_heads = jnp.einsum(
            "shij,sjhd->ihd", probs_low, near_values, preferred_element_type=jnp.float32
        ).astype(jnp.bfloat16)
        grad_probs = jnp.einsum(
            "ihd,sjhd->shij", cot_rows, near_values, preferred_element_type=jnp.float32
        )
        row_total = jnp.sum(probabilities * grad_probs, axis=(0, 3), keepdims=True)
        grad_scores = (probabilities * (grad_probs - row_total)).astype(jnp.bfloat16)
        return (mixed_heads.reshape(block_size, width_part), grad_scores)

    mixed_rows, grad_blocks = jax.vmap(attend_row)(
        queries, cot_heads, bias_chan, own_cols, own_chain, own_mask
    )
    node_rows = block_rows * block_size // rows_split
    mixed_nodes = mixed_rows.reshape(block_rows * block_size, width_part)
    summed = lax.psum_scatter(
        jnp.dot(mixed_nodes, out_weight, preferred_element_type=jnp.float32).astype(jnp.bfloat16),
        "row",
        scatter_dimension=0,
        tiled=True,
    ).astype(jnp.float32)
    own_nodes = lax.dynamic_slice_in_dim(node_feats, row_index * node_rows, node_rows, 0)
    node_out = (own_nodes.astype(jnp.float32) + summed).astype(jnp.bfloat16)
    tri_rows, grad_rows = (
        lax.all_to_all(tri_chan, "row", split_axis=3, concat_axis=2, tiled=True),
        lax.all_to_all(grad_blocks, "row", split_axis=3, concat_axis=2, tiled=True),
    )
    tri_norm = norm_parts(tri_rows.astype(jnp.float32), 2)[0].astype(jnp.bfloat16)
    update = jnp.einsum(
        "rsxij,xc->rsijc", tri_norm, tri_out_weight, preferred_element_type=jnp.float32
    )
    pair_out = (pair_float + gate_values.astype(jnp.float32) * update).astype(jnp.bfloat16)
    grad_normed = jnp.einsum(
        "rshij,ch->rsijc", grad_rows, bias_weight, preferred_element_type=jnp.float32
    )
    centre_grad = grad_normed - jnp.mean(grad_normed, axis=4, keepdims=True)
    projection_mean = jnp.mean(grad_normed * normed, axis=4, keepdims=True)
    pair_grad = (pair_scale * (centre_grad - normed * projection_mean)).astype(jnp.bfloat16)
    return (pair_out, node_out, pair_grad)


def solution(mesh):
    in_specs = (
        P("grp", None, "row", None, None),
        P(),
        P(),
        P(),
        P(),
        P("grp", None),
        P("grp", None),
        P(),
        P(),
        P(),
        P(),
        P(None, "row"),
        P(None, "row"),
        P(None, "row"),
        P("row", None),
    )
    out_specs = (
        P("grp", None, "row", None, None),
        P(("grp", "row"), None),
        P("grp", None, "row", None, None),
    )
    return jax.shard_map(
        per_device, mesh=mesh, in_specs=in_specs, out_specs=out_specs, check_vma=False
    )
```

profile of v0, /device:TPU:1, one launch (start us, length us, event | category | flops | bytes accessed | tf_op | source)
XLA Modules:
  0.0 657.0 jit_solution(987476454767488791)
XLA Ops:
  11.9 7.3 %fusion.14 = f32[4,6,8,128]{3,2,1,0:T(8,128)S(1)} fusion(bf16[4,6,8,128,128]{4,3,2,1,0:T(8,128)(2,1)S(1)} %copy-done.3, f32[4,6,8,128]{3,2,1,0:T(8,128)S(1)} %broadcast_multiply_fusion.3), kind=kLoop, calls=%fused_computation.25 | loop fusion | flops 12558336 | bytes 6488064 | tf_op jit(solution)/shard_map/reduce_sum | solution.py:15
  19.3 9.6 %fusion.56 = bf16[4,6,16,8,128]{4,2,3,1,0:T(8,128)(2,1)S(1)} fusion(bf16[4,6,8,128,128]{4,3,2,1,0:T(8,128)(2,1)S(1)} %copy-done.3, f32[4,6,8,128]{3,2,1,0:T(8,128)S(1)} %add_rsqrt_fusion.1, f32[4,6,8,128]{3,2,1,0:T(8,128)S(1)} %broadcast_multiply_fusion.3, bf16[128,16]{0,1:T(8,128)(2,1)S(1)} %copy-done.26), kind=kOutput, calls=%fused_computation.76 | convolution fusion | flops 113639424 | bytes 7278592 | tf_op jit(solution)/shard_map/rsijc,ch->rshij/dot_general | solution.py:69
  30.0 8.6 %all-to-all-start.5 = ((bf16[4,6,16,8,128]{4,3,1,0,2:T(8,128)(2,1)}), bf16[4,6,16,8,128]{4,3,1,0,2:T(8,128)(2,1)S(1)}, u32[]{:S(2)}, u32[]{:S(2)}) async-start(bf16[4,6,16,8,128]{4,3,1,0,2:T(8,128)(2,1)} %copy.271), calls=%async_computation.5 | async-start | bytes 1572864 | tf_op jit(solution)/shard_map/all_to_all | solution.py:75
  39.5 13.9 %fusion.34 = f32[4,6,8,128,256]{4,3,2,1,0:T(8,128)} fusion(bf16[4,6,8,128,128]{4,3,2,1,0:T(8,128)(2,1)} %param.17, f32[4,6,8,128]{3,2,1,0:T(8,128)S(1)} %add_rsqrt_fusion.1, f32[4,6,8,128]{3,2,1,0:T(8,128)S(1)} %broadcast_multiply_fusion.3, bf16[128,256]{1,0:T(8,128)(2,1)S(1)} %copy-done.18), kind=kOutput, calls=%fused_computation.55 | convolution fusion | flops 1623195648 | bytes 31719424 | tf_op jit(solution)/shard_map/rsijc,cx->rsxij/dot_general | solution.py:57
  53.3 24.7 %copy.247 = f32[4,6,8,128,256]{3,2,4,1,0:T(8,128)} copy(f32[4,6,8,128,256]{4,3,2,1,0:T(8,128)} %fusion.34) | data formatting | bytes 50331648 | tf_op jit(solution)/shard_map/rsijc,cx->rsxij/dot_general | solution.py:57
  78.0 11.6 %fusion.21 = (bf16[4,6,64,8,128]{4,3,2,1,0:T(8,128)(2,1)S(1)}, bf16[4,6,64,8,128]{4,3,2,1,0:T(8,128)(2,1)}) fusion(f32[4,6,256,8,128]{4,3,2,1,0:T(8,128)} %bitcast.184), kind=kLoop, calls=%fused_computation.37 | loop fusion | flops 15728640 | bytes 31457280 | tf_op jit(solution)/shard_map/convert_element_type | solution.py:65
  111.8 134.2 %all-to-all-done.1 = bf16[8,2,6,64,8,128]{5,4,3,2,1,0:T(8,128)(2,1)} async-done(((bf16[8,2,6,64,8,128]{5,4,3,2,1,0:T(8,128)(2,1)}), bf16[8,2,6,64,8,128]{5,4,3,2,1,0:T(8,128)(2,1)}, u32[]{:S(2)}, u32[]{:S(2)}) %all-to-all-start.1) | async-done | bytes 12582944 | tf_op jit(solution)/shard_map/all_to_all | solution.py:101
  246.0 7.5 %all-to-all-start = ((bf16[4,6,64,8,128]{4,3,1,0,2:T(8,128)(2,1)}), bf16[4,6,64,8,128]{4,3,1,0,2:T(8,128)(2,1)}, u32[]{:S(2)}, u32[]{:S(2)}) async-start(bf16[4,6,64,8,128]{4,3,1,0,2:T(8,128)(2,1)} %copy.248), calls=%async_computation | async-start | bytes 6291456 | tf_op jit(solution)/shard_map/all_to_all | solution.py:74
  253.4 24.9 %copy.255 = bf16[8,2,6,64,8,128]{5,0,4,2,1,3:T(8,128)(2,1)} copy(bf16[8,2,6,64,8,128]{5,4,3,2,1,0:T(8,128)(2,1)} %all-to-all-done.1) | data formatting | bytes 25165824 | tf_op jit(solution)/shard_map/all_to_all | solution.py:101
  278.3 21.4 %all-to-all-done = bf16[4,6,64,8,128]{4,3,1,0,2:T(8,128)(2,1)} async-done(((bf16[4,6,64,8,128]{4,3,1,0,2:T(8,128)(2,1)}), bf16[4,6,64,8,128]{4,3,1,0,2:T(8,128)(2,1)}, u32[]{:S(2)}, u32[]{:S(2)}) %all-to-all-start) | async-done | bytes 3145760 | tf_op jit(solution)/shard_map/all_to_all | solution.py:74
  308.7 14.9 %all_gather.7 = bf16[4096,48]{0,1:T(8,128)(2,1)S(1)} all-gather(bf16[512,48]{0,1:T(8,128)(2,1)S(1)} %convolution_convert_fusion.4), channel_id=1, replica_groups=mesh['grp'=8,'row'=16] {'grp'}, dimensions={0}, use_global_device_ids=true | all-gather | bytes 442368 | tf_op jit(solution)/shard_map/all_gather | solution.py:137
  326.8 13.0 %all_gather.6 = bf16[4096,48]{0,1:T(8,128)(2,1)S(1)} all-gather(bf16[512,48]{0,1:T(8,128)(2,1)S(1)} %convolution_convert_fusion.5), channel_id=1, replica_groups=mesh['grp'=8,'row'=16] {'grp'}, dimensions={0}, use_global_device_ids=true | all-gather | bytes 442368 | tf_op jit(solution)/shard_map/all_gather | solution.py:138
  350.9 12.9 %fusion.36 = f32[4,6,8,128,128]{4,3,2,1,0:T(8,128)} fusion(bf16[4,6,8,128,128]{4,3,2,1,0:T(8,128)(2,1)} %param.17, f32[4,6,8,128]{3,2,1,0:T(8,128)S(1)} %add_rsqrt_fusion.1, f32[4,6,8,128]{3,2,1,0:T(8,128)S(1)} %broadcast_multiply_fusion.3, bf16[128,128]{1,0:T(8,128)(2,1)S(1)} %copy-done.20), kind=kOutput, calls=%fused_computation.56 | convolution fusion | flops 817889280 | bytes 19103744 | tf_op jit(solution)/shard_map/rsijc,cy->rsijy/dot_general | solution.py:67
  376.9 111.5 %all-to-all-done.2 = bf16[8,2,6,64,8,128]{5,0,4,2,1,3:T(8,128)(2,1)} async-done(((bf16[8,2,6,64,8,128]{5,0,4,2,1,3:T(8,128)(2,1)}), bf16[8,2,6,64,8,128]{5,0,4,2,1,3:T(8,128)(2,1)}, u32[]{:S(2)}, u32[]{:S(2)}) %all-to-all-start.2) | async-done | bytes 12582944 | tf_op jit(solution)/shard_map/all_to_all | solution.py:100
  494.2 7.6 %copy.257 = bf16[8,2,6,4,16,8,128]{6,5,4,3,2,1,0:T(8,128)(2,1)S(1)} copy(bf16[8,2,6,4,16,8,128]{6,0,5,2,1,3,4:T(8,128)(2,1)} %bitcast.19) | data formatting | bytes 25165824 | tf_op jit(solution)/shard_map/all_to_all | solution.py:100
  508.4 13.9 %gather_fusion.2 = bf16[24,6,4,128,128]{4,3,2,1,0:T(8,128)(2,1)} fusion(bf16[20,6,4,128,128]{4,3,2,1,0:T(8,128)(2,1)} %pad_maximum_fusion, s32[1024]{0:T(1024)S(1)} %pad_clamp_fusion), kind=kCustom, calls=%fused_computation.4 | custom fusion | bytes 37748832 | tf_op jit(solution)/shard_map/vmap(jit(_take))/gather | solution.py:115
  522.3 23.4 %fusion.9 = bf16[4,6,6,4,128,128]{5,2,4,3,1,0:T(8,128)(2,1)} fusion(bf16[4,6,6,4,128,128]{5,4,3,2,1,0:T(8,128)(2,1)} %bitcast.187, pred[4,6]{1,0:T(4,128)(4,1)S(1)} %copy-done.28, s32[4,6,6]{2,1,0:T(8,128)S(1)} %copy-done.21, s32[4,6]{1,0:T(4,128)S(1)} %copy-done.23), kind=kOutput, calls=%fused_computation.20 | convolution fusion | flops 132121440 | bytes 37749432 | tf_op jit(solution)/shard_map/vmap(stu,sudjk->stdjk)/dot_general | solution.py:118
  545.7 6.7 %all-to-all-start.6 = ((bf16[4,6,1,128,128]{4,0,2,1,3:T(4,128)(2,1)}), bf16[4,6,1,128,128]{4,0,2,1,3:T(4,128)(2,1)S(1)}, u32[]{:S(2)}, u32[]{:S(2)}) async-start(bf16[4,6,1,128,128]{4,0,2,1,3:T(4,128)(2,1)} %copy.277), calls=%async_computation.7 | async-start | bytes 1572864 | tf_op jit(solution)/shard_map/all_to_all | solution.py:195
  552.4 13.0 %fusion.25 = bf16[4,6,4,128,128]{3,4,1,2,0:T(8,128)(2,1)} fusion(bf16[4,6,4,16,8,128]{5,4,1,0,2,3:T(8,128)(2,1)} %bitcast.24, bf16[4,6,6,4,128,128]{5,2,4,3,1,0:T(8,128)(2,1)} %fusion.9), kind=kOutput, calls=%fused_computation.46 | convolution fusion | flops 2417491968 | bytes 25165824 | tf_op jit(solution)/shard_map/vmap(tdik,stdjk->sdij)/dot_general | solution.py:121
  571.6 6.9 %all-to-all-start.4 = ((bf16[4,6,4,128,128]{4,2,1,0,3:T(4,128)(2,1)}), bf16[4,6,4,128,128]{4,2,1,0,3:T(4,128)(2,1)}, u32[]{:S(2)}, u32[]{:S(2)}) async-start(bf16[4,6,4,128,128]{4,2,1,0,3:T(4,128)(2,1)} %copy.263), calls=%async_computation.4 | async-start | bytes 6291456 | tf_op jit(solution)/shard_map/all_to_all | solution.py:194
  584.9 12.6 %copy.280 = f32[4,6,8,128,128]{4,3,2,1,0:T(8,128)} copy(f32[4,6,8,128,128]{3,4,2,1,0:T(8,128)} %get-tuple-element.19) | data formatting | bytes 25165824 | tf_op jit(solution)/shard_map/rshij,ch->rsijc/dot_general | solution.py:202
  597.5 13.3 %fusion.10 = f32[4,6,8,128]{3,2,1,0:T(8,128)S(1)} fusion(f32[4,6,8,128,128]{4,3,2,1,0:T(8,128)} %copy.280, bf16[4,6,8,128,128]{4,3,2,1,0:T(8,128)(2,1)} %param.17, f32[4,6,8,128]{3,2,1,0:T(8,128)S(1)} %copy-done.11, f32[4,6,8,128]{3,2,1,0:T(8,128)S(1)} %broadcast_multiply_fusion.3), kind=kLoop, calls=%fused_computation.21 | loop fusion | flops 15704064 | bytes 19169280 | tf_op jit(solution)/shard_map/reduce_sum | solution.py:206
  610.8 18.2 %fusion.13 = bf16[4,6,8,128,128]{4,3,2,1,0:T(8,128)(2,1)} fusion(bf16[4,6,8,128,128]{4,3,2,1,0:T(8,128)(2,1)} %param.17, f32[4,6,8,128,128]{4,3,2,1,0:T(8,128)S(1)} %copy-done.4, f32[4,6,8,128]{3,2,1,0:T(8,128)S(1)} %get-tuple-element.22, f32[4,6,8,128]{3,2,1,0:T(8,128)S(1)} %get-tuple-element.23, f32[4,6,8,128]{3,2,1,0:T(8,128)S(1)} %copy-done.11, ...), kind=kLoop, calls=%fused_computation.24 | loop fusion | flops 25165824 | bytes 25559040 | tf_op jit(solution)/shard_map/convert_element_type | solution.py:207
  641.2 8.7 %fusion.15 = bf16[4,6,8,128,128]{4,3,2,1,0:T(8,128)(2,1)} fusion(bf16[4,6,8,128,128]{4,3,2,1,0:T(8,128)(2,1)S(1)} %bitcast.183, f32[4,6,8,128,128]{4,3,2,1,0:T(8,128)} %fusion.36, bf16[4,6,64,8,128]{4,3,2,1,0:T(8,128)(2,1)S(1)} %multiply_convert_fusion, bf16[64,128]{1,0:T(8,128)(2,1)S(1)} %copy-done.30), kind=kOutput, calls=%fused_computation.26 | convolution fusion | flops 430964736 | bytes 28327936 | tf_op jit(solution)/shard_map/rsxij,xc->rsijc/dot_general | solution.py:198
  (162 shorter events, 102.0 us)
Async XLA Ops:
  7.2 334.1 %copy-start = (bf16[512,768]{1,0:T(8,128)(2,1)S(1)}, bf16[512,768]{1,0:T(8,128)(2,1)}, u32[]{:S(2)}) copy-start(bf16[512,768]{1,0:T(8,128)(2,1)} %param.23) | copy-start | bytes 2359300
  19.3 331.7 %copy-start.10 = (f32[4,6,8,128]{3,2,1,0:T(8,128)}, f32[4,6,8,128]{3,2,1,0:T(8,128)S(1)}, u32[]{:S(2)}) copy-start(f32[4,6,8,128]{3,2,1,0:T(8,128)S(1)} %add_rsqrt_fusion.1) | copy-start | bytes 294916
  19.3 19.4 %copy-start.24 = (s32[32,6]{0,1:T(8,128)S(1)}, s32[32,6]{0,1:T(8,128)}, u32[]{:S(2)}) copy-start(s32[32,6]{0,1:T(8,128)} %param.18) | copy-start | bytes 2308
  19.3 20.2 %copy-start.18 = (bf16[128,256]{1,0:T(8,128)(2,1)S(1)}, bf16[128,256]{1,0:T(8,128)(2,1)}, u32[]{:S(2)}) copy-start(bf16[128,256]{1,0:T(8,128)(2,1)} %param.24) | copy-start | bytes 196612
  30.0 70.2 %all-to-all-start.5 = ((bf16[4,6,16,8,128]{4,3,1,0,2:T(8,128)(2,1)}), bf16[4,6,16,8,128]{4,3,1,0,2:T(8,128)(2,1)S(1)}, u32[]{:S(2)}, u32[]{:S(2)}) async-start(bf16[4,6,16,8,128]{4,3,1,0,2:T(8,128)(2,1)} %copy.271), calls=%async_computation.5 | async-start | bytes 1572864 | tf_op jit(solution)/shard_map/all_to_all | solution.py:75
  101.1 144.9 %all-to-all-start.1 = ((bf16[8,2,6,64,8,128]{5,4,3,2,1,0:T(8,128)(2,1)}), bf16[8,2,6,64,8,128]{5,4,3,2,1,0:T(8,128)(2,1)}, u32[]{:S(2)}, u32[]{:S(2)}) async-start(bf16[8,2,6,64,8,128]{5,4,3,2,1,0:T(8,128)(2,1)} %copy.254), calls=%async_computation.1 | async-start | bytes 25165824 | tf_op jit(solution)/shard_map/all_to_all | solution.py:101
  246.0 53.7 %all-to-all-start = ((bf16[4,6,64,8,128]{4,3,1,0,2:T(8,128)(2,1)}), bf16[4,6,64,8,128]{4,3,1,0,2:T(8,128)(2,1)}, u32[]{:S(2)}, u32[]{:S(2)}) async-start(bf16[4,6,64,8,128]{4,3,1,0,2:T(8,128)(2,1)} %copy.248), calls=%async_computation | async-start | bytes 6291456 | tf_op jit(solution)/shard_map/all_to_all | solution.py:74
  278.3 27.1 %copy-start.2 = (s32[32]{0:T(128)S(1)}, s32[32]{0:T(128)}, u32[]{:S(2)}) copy-start(s32[32]{0:T(128)} %param.20) | copy-start | bytes 388
  278.3 29.1 %copy-start.7 = (bf16[512,768]{1,0:T(8,128)(2,1)S(1)}, bf16[512,768]{1,0:T(8,128)(2,1)}, u32[]{:S(2)}) copy-start(bf16[512,768]{1,0:T(8,128)(2,1)} %param.22) | copy-start | bytes 2359300
  278.3 29.9 %copy-start.16 = (bf16[768,48]{0,1:T(8,128)(2,1)S(1)}, bf16[768,48]{0,1:T(8,128)(2,1)}, u32[]{:S(2)}) copy-start(bf16[768,48]{0,1:T(8,128)(2,1)} %param.29) | copy-start | bytes 221188
  299.7 188.7 %all-to-all-start.2 = ((bf16[8,2,6,64,8,128]{5,0,4,2,1,3:T(8,128)(2,1)}), bf16[8,2,6,64,8,128]{5,0,4,2,1,3:T(8,128)(2,1)}, u32[]{:S(2)}, u32[]{:S(2)}) async-start(bf16[8,2,6,64,8,128]{5,0,4,2,1,3:T(8,128)(2,1)} %copy.255), calls=%async_computation.2 | async-start | bytes 25165824 | tf_op jit(solution)/shard_map/all_to_all | solution.py:100
  304.7 19.7 %copy-start.25 = (s32[32,6]{0,1:T(8,128)S(1)}, s32[32,6]{0,1:T(8,128)}, u32[]{:S(2)}) copy-start(s32[32,6]{0,1:T(8,128)} %param.19) | copy-start | bytes 2308
  304.7 19.8 %copy-start.17 = (bf16[768,48]{0,1:T(8,128)(2,1)S(1)}, bf16[768,48]{0,1:T(8,128)(2,1)}, u32[]{:S(2)}) copy-start(bf16[768,48]{0,1:T(8,128)(2,1)} %param.28) | copy-start | bytes 221188
  304.7 324.3 %reduce-scatter.2.cloned.1.call-start = ((), (), s32[]{:S(2)}) async-start(), calls=%async_computation.8 | async-start | bytes 835584 | tf_op jit(solution)/shard_map/reduce_scatter | solution.py:185
  307.6 33.7 %copy-start.14 = (bf16[48,768]{1,0:T(8,128)(2,1)S(1)}, bf16[48,768]{1,0:T(8,128)(2,1)}, u32[]{:S(2)}) copy-start(bf16[48,768]{1,0:T(8,128)(2,1)} %param.31) | copy-start | bytes 221188
  308.6 34.5 %copy-start.31 = (f32[16]{0:T(128)S(1)}, f32[16]{0:T(128)}, u32[]{:S(2)}) copy-start(f32[16]{0:T(128)} %param.21) | copy-start | bytes 196
  308.6 35.0 %copy-start.22 = (s32[4,6]{1,0:T(4,128)S(1)}, s32[4,6]{1,0:T(4,128)}, u32[]{:S(2)}) copy-start(s32[4,6]{1,0:T(4,128)} %get-tuple-element.9) | copy-start | bytes 292
  308.6 35.0 %copy-start.29 = (s32[4]{0:T(128)S(1)}, s32[4]{0:T(128)}, u32[]{:S(2)}) copy-start(s32[4]{0:T(128)} %dynamic_slice.31) | copy-start | bytes 52
  488.4 57.3 %all-to-all-start.3 = ((bf16[4,6,64,8,128]{4,3,1,0,2:T(8,128)(2,1)}), bf16[4,6,64,8,128]{4,3,1,0,2:T(8,128)(2,1)}, u32[]{:S(2)}, u32[]{:S(2)}) async-start(bf16[4,6,64,8,128]{4,3,1,0,2:T(8,128)(2,1)} %copy.259), calls=%async_computation.3 | async-start | bytes 6291456 | tf_op jit(solution)/shard_map/all_to_all | solution.py:73
  508.4 13.9 %copy-start.21 = (s32[4,6,6]{2,1,0:T(8,128)S(1)}, s32[4,6,6]{2,1,0:T(8,128)}, u32[]{:S(2)}) copy-start(s32[4,6,6]{2,1,0:T(8,128)} %copy.243) | copy-start | bytes 1732
  508.4 13.9 %copy-start.23 = (s32[4,6]{1,0:T(4,128)S(1)}, s32[4,6]{1,0:T(4,128)}, u32[]{:S(2)}) copy-start(s32[4,6]{1,0:T(4,128)} %get-tuple-element.9) | copy-start | bytes 292
  508.4 13.9 %copy-start.28 = (pred[4,6]{1,0:T(4,128)(4,1)S(1)}, pred[4,6]{1,0:T(4,128)(4,1)}, u32[]{:S(2)}) copy-start(pred[4,6]{1,0:T(4,128)(4,1)} %get-tuple-element.6) | copy-start | bytes 76
  545.7 25.9 %all-to-all-start.6 = ((bf16[4,6,1,128,128]{4,0,2,1,3:T(4,128)(2,1)}), bf16[4,6,1,128,128]{4,0,2,1,3:T(4,128)(2,1)S(1)}, u32[]{:S(2)}, u32[]{:S(2)}) async-start(bf16[4,6,1,128,128]{4,0,2,1,3:T(4,128)(2,1)} %copy.277), calls=%async_computation.7 | async-start | bytes 1572864 | tf_op jit(solution)/shard_map/all_to_all | solution.py:195
  571.6 58.8 %all-to-all-start.4 = ((bf16[4,6,4,128,128]{4,2,1,0,3:T(4,128)(2,1)}), bf16[4,6,4,128,128]{4,2,1,0,3:T(4,128)(2,1)}, u32[]{:S(2)}, u32[]{:S(2)}) async-start(bf16[4,6,4,128,128]{4,2,1,0,3:T(4,128)(2,1)} %copy.263), calls=%async_computation.4 | async-start | bytes 6291456 | tf_op jit(solution)/shard_map/all_to_all | solution.py:194
  (18 other events, 119.9 us)
Sparse Core Ops, SparseCore 0:
  372.5 173.2 reduce-scatter.1
where the time goes:
time: 670 us; the launch traced here: 657 us
  waiting for transfers between devices  267 us (40%)
  local copies, waits for them, and re-layouts  125 us (19%)
  matrix products  98.7 us (15%)
  other arithmetic  77.1 us (12%)
  starting transfers between devices  46.8 us (7%)
  blocking collectives  27.9 us (4%)
  between operations  14.9 us (2%)
    all_to_all x1, waiting for transfers between devices, per_device(): lax.all_to_all(outgoing, 'grp', split_axis=0, concat_axis=0, tiled=True)  134 us
    all_to_all x1, waiting for transfers between devices, per_device(): lax.all_to_all(lax.all_to_all(outgoing, 'grp', split_axis=0, concat_axis=...  111 us
    all_to_all x1, local copies, waits for them, and re-layouts, per_device(): lax.all_to_all(outgoing, 'grp', split_axis=0, concat_axis=0, tiled=True)  24.9 us
    dot_general x1, local copies, waits for them, and re-layouts, per_device(): jnp.einsum('rsijc,cx->rsxij', normed_short, tri_weight, preferred_element...  24.7 us
    dot_general x1, matrix products, triangle_row(): jnp.einsum('stu,sudjk->stdjk', matches, far_rows, preferred_element_type=...  23.4 us
    all_to_all x1, waiting for transfers between devices, per_device(): lax.all_to_all(right_proj, 'row', split_axis=2, concat_axis=3, tiled=True)  21.4 us
    convert_element_type x1, other arithmetic, per_device(): (pair_scale * (centre_grad - normed * projection_mean)).astype(jnp.bfloat16)  18.2 us
    all_gather x1, blocking collectives, per_device(): lax.all_gather(keys_here, 'grp', axis=0, tiled=True)  14.9 us
  transfers between devices with their start and end apart: 8, of which 3 were waited for; matrix products, arithmetic and copies ran while one was open for 39% of the time, Pallas kernels for 0%

commit v1 on v0

v1 whole, which is shorter than its diff:
```python
import jax
import jax.numpy as jnp
from jax import lax
from jax.experimental import pallas as pl
from jax.experimental.pallas import tpu as pltpu
from jax.sharding import PartitionSpec as P

F32 = jnp.float32
BF16 = jnp.bfloat16
MESH = pl.DeviceIdType.MESH
EPS = 1e-5
GRP, ROW = 8, 16
BR, KS, BLK, CZ, CH = 4, 6, 128, 128, 64
NB = BR * KS
QC = CH // ROW
PAD = 128
VOFF = 64
ROW_ORDER = (1, 3, 4, 12, 2, 8, 5, 15, 7, 13, 6, 14, 9, 11, 10)
GRP_ORDER = (2, 6, 4, 3, 7, 5, 1)


def row_peer(row, offset):
    z, y = row // 4, row % 4
    return ((z + offset // 4) % 4) * 4 + (y + offset % 4) % 4


def grp_peer(grp, offset):
    x, core = grp // 2, grp % 2
    return ((x + offset // 2) % 4) * 2 + (core + offset % 2) % 2


def layer_norm(values):
    center = jnp.mean(values, axis=-1, keepdims=True)
    shifted = values - center
    spread = jnp.mean(shifted * shifted, axis=-1, keepdims=True)
    inverse = lax.rsqrt(spread + EPS)
    return shifted * inverse, inverse


def dot_nt(a, b):
    return lax.dot_general(a, b, (((1,), (1,)), ((), ())), preferred_element_type=F32)


def dot_nn(a, b):
    return lax.dot_general(a, b, (((1,), (0,)), ((), ())), preferred_element_type=F32)


def dot_tn(a, b):
    return lax.dot_general(a, b, (((0,), (0,)), ((), ())), preferred_element_type=F32)


def i32(flag):
    return jnp.where(flag, 1, 0).astype(jnp.int32)


def named_ranks(cols, reader, owner):
    flags = [jnp.int32(0)] * BR
    for r in range(BR):
        for s in range(KS):
            c = cols[reader * BR + r, s]
            for l in range(BR):
                flags[l] = flags[l] | i32(c == owner * BR + l)
    ranks, count = [], jnp.int32(0)
    firsts = [jnp.int32(0), jnp.int32(0)]
    for l in range(BR):
        ranks.append(count)
        for a in range(2):
            firsts[a] = firsts[a] + l * flags[l] * i32(count == a)
        count = count + flags[l]
    return ranks, firsts


def pick(entries, index):
    out = jnp.int32(0)
    for n, entry in enumerate(entries):
        out = out + entry * i32(index == n)
    return out


def write_tables(cols, grp, step, place, kvplace, stage, kvstage):
    inner = step // KS
    slot = step % KS
    j = cols[grp * BR + inner, slot]
    owner = j >> 2
    own = owner == grp
    ranks, _ = named_ranks(cols, grp, owner)
    offset = ((grp // 2 - owner // 2 + 4) % 4) * 2 + (grp % 2 - owner % 2 + 2) % 2
    rank_j = pick(ranks, j & 3)
    theirs = [cols[j, u] for u in range(KS)]
    for t in range(KS):
        c = cols[grp * BR + inner, t]
        found, far, count = jnp.int32(-1), jnp.int32(0), jnp.int32(0)
        for u in range(KS):
            hit = theirs[u] == c
            found = jnp.where(hit, u, found)
            far = jnp.where(hit, count, far)
            count = count + i32((theirs[u] >> 2) != owner)
        n = jnp.where((c >> 2) == owner, pick(ranks, c & 3), 2 + far)
        remote = NB + (offset - 1) * 8 + rank_j * 4 + n
        place[step * KS + t] = jnp.where(
            found >= 0, jnp.where(own, (j & 3) * KS + found, remote), NB + 56
        )
    kvplace[step] = jnp.where(own, j & 3, BR + (offset - 1) * 2 + rank_j)
    to = 1 + step % 7
    reader = grp_peer(grp, to)
    _, firsts = named_ranks(cols, reader, grp)
    for a in range(2):
        near, far = [jnp.int32(0)] * 2, [jnp.int32(0)] * 2
        count = jnp.int32(0)
        for u in range(KS):
            c = cols[grp * BR + firsts[a], u]
            away = i32((c >> 2) != grp)
            for n in range(2):
                near[n] = near[n] + u * i32(c == grp * BR + firsts[n])
                far[n] = far[n] + u * away * i32(count == n)
            count = count + away
        for n in range(2):
            stage[(to - 1) * 8 + a * 4 + n] = firsts[a] * KS + near[n]
            stage[(to - 1) * 8 + a * 4 + 2 + n] = firsts[a] * KS + far[n]
        kvstage[(to - 1) * 2 + a] = firsts[a]


def project_kernel(
    cols, pair, tri_w, bias_w, left, right, bias, place, kvplace, stage, kvstage, weights, turned
):
    grp = lax.axis_index("grp")
    step = pl.program_id(0)

    @pl.when(step == 0)
    def _():
        weights[: 4 * CH, :] = tri_w[...].astype(F32).T.astype(BF16)
        weights[4 * CH :, :] = bias_w[...]

    write_tables(cols, grp, step, place, kvplace, stage, kvstage)
    for i in range(8):
        normed = layer_norm(pair[0, i].astype(F32))[0].astype(BF16)
        projected = dot_nt(weights[...], normed)
        turned[pl.ds(i, CH, stride=8), :] = (
            jax.nn.sigmoid(projected[CH : 2 * CH]) * projected[:CH]
        )
        turned[pl.ds(8 * CH + i, CH, stride=8), :] = (
            jax.nn.sigmoid(projected[3 * CH : 4 * CH]) * projected[2 * CH : 3 * CH]
        )
        turned[pl.ds(16 * CH + i, ROW, stride=8), :] = projected[4 * CH :]
    left[:, 0] = turned[: 8 * CH].reshape(CH, 8, BLK).astype(BF16)
    right[:, 0] = turned[8 * CH : 16 * CH].reshape(CH, 8, BLK).astype(BF16)
    bias[:, 0] = turned[16 * CH :].reshape(ROW, 8, BLK).astype(BF16)


def project(cols, pair, tri_w, bias_w):
    smem = pl.BlockSpec(memory_space=pltpu.SMEM)
    by_block = lambda n: pl.BlockSpec((n, 1, 8, BLK), lambda b: (0, b, 0, 0))
    whole = lambda a: pl.BlockSpec(a.shape, lambda b: (0,) * a.ndim)
    return pl.pallas_call(
        project_kernel,
        grid=(NB,),
        in_specs=[
            smem,
            pl.BlockSpec((1, 8, BLK, CZ), lambda b: (b, 0, 0, 0)),
            whole(tri_w),
            whole(bias_w),
        ],
        out_specs=[by_block(CH), by_block(CH), by_block(ROW), smem, smem, smem, smem],
        out_shape=[
            jax.ShapeDtypeStruct((CH, NB, 8, BLK), BF16),
            jax.ShapeDtypeStruct((CH, NB, 8, BLK), BF16),
            jax.ShapeDtypeStruct((ROW, NB, 8, BLK), BF16),
            jax.ShapeDtypeStruct((NB * KS,), jnp.int32),
            jax.ShapeDtypeStruct((NB,), jnp.int32),
            jax.ShapeDtypeStruct((56,), jnp.int32),
            jax.ShapeDtypeStruct((14,), jnp.int32),
        ],
        scratch_shapes=[
            pltpu.VMEM((4 * CH + ROW, CZ), BF16),
            pltpu.VMEM(((2 * CH + ROW) * 8, BLK), F32),
        ],
        compiler_params=pltpu.CompilerParams(vmem_limit_bytes=40 << 20),
        name="project",
    )(cols, pair, tri_w, bias_w)


def exchange_kernel(*refs):
    (
        cols, mask, chain, same, place, kvplace, stage, kvstage,
        left_in, right_in, bias_in, nodes, cotan, q_w, k_w, v_w, o_w,
        tri_out, grad_out, node_out,
    ) = refs[:20]
    scr = list(refs[20:])
    take = lambda n: [scr.pop(0) for _ in range(n)]
    right = take(QC)
    left = take(QC)
    tri = take(QC)
    xs = take(QC)
    xr = take(QC)
    (bias, grads, kv_own, kv_s, kv_r, kv_all, queries, cots, mixed, mixed_r, wo_all,
     wq_pad, wkv_pad, wo_pad, scores, gprobs) = take(16)
    (right_ss, right_rs, left_ss, left_rs, tri_ss, tri_rs, x_ss, x_rs,
     kv_ss, kv_rs, bias_ss, bias_rs, grad_ss, grad_rs, mix_ss, mix_rs, wo_ss, wo_rs, own_s) = take(19)

    grp = lax.axis_index("grp")
    row = lax.axis_index("row")
    mine = pl.ds(pl.multiple_of(row * 8, 8), 8)

    def to_row(src, dst, ss, rs, peer):
        return pltpu.make_async_remote_copy(
            src, dst, ss, rs, device_id=(grp, peer), device_id_type=MESH
        )

    def to_grp(src, dst, ss, rs, peer):
        return pltpu.make_async_remote_copy(
            src, dst, ss, rs, device_id=(peer, row), device_id_type=MESH
        )

    wo_all[...] = jnp.zeros_like(wo_all)
    wo_pad[...] = jnp.zeros_like(wo_pad)

    barrier = pltpu.get_barrier_semaphore()
    for offset in ROW_ORDER:
        pl.semaphore_signal(barrier, inc=1, device_id=(grp, row_peer(row, offset)), device_id_type=MESH)
    for offset in GRP_ORDER:
        pl.semaphore_signal(barrier, inc=1, device_id=(grp_peer(grp, offset), row), device_id_type=MESH)
    pl.semaphore_wait(barrier, 22)

    peers = [row_peer(row, offset) for offset in ROW_ORDER]

    bias_c = [
        to_row(bias_in.at[p], bias.at[:, mine, :], bias_ss.at[n], bias_rs.at[n], p)
        for n, p in enumerate(peers)
    ]
    right_c = [
        [
            to_row(right_in.at[q * ROW + p], right[q].at[:, mine, :], right_ss.at[q, n], right_rs.at[q, n], p)
            for n, p in enumerate(peers)
        ]
        for q in range(QC)
    ]
    left_c = [
        [
            to_row(left_in.at[q * ROW + p], left[q].at[:, mine, :], left_ss.at[q, n], left_rs.at[q, n], p)
            for n, p in enumerate(peers)
        ]
        for q in range(QC)
    ]
    wo_c = [
        to_row(o_w, wo_all.at[row, pl.ds(VOFF, 48), :], wo_ss.at[n], wo_rs.at[n], p)
        for n, p in enumerate(peers)
    ]
    own_c = (
        [pltpu.make_async_copy(right_in.at[q * ROW + row], right[q].at[:, mine, :], own_s.at[q]) for q in range(QC)]
        + [pltpu.make_async_copy(left_in.at[q * ROW + row], left[q].at[:, mine, :], own_s.at[QC + q]) for q in range(QC)]
        + [pltpu.make_async_copy(bias_in.at[row], bias.at[:, mine, :], own_s.at[2 * QC])]
        + [pltpu.make_async_copy(o_w, wo_all.at[row, pl.ds(VOFF, 48), :], own_s.at[2 * QC + 1])]
    )
    for c in right_c[0]:
        c.start()
    for c in own_c:
        c.start()
    for q in range(1, QC):
        for c in right_c[q]:
            c.start()
    for c in bias_c:
        c.start()
    for q in range(QC):
        for c in left_c[q]:
            c.start()
    for c in wo_c:
        c.start()

    wq_pad[...] = jnp.zeros_like(wq_pad)
    wkv_pad[...] = jnp.zeros_like(wkv_pad)
    wq_pad[:, :48] = q_w[...]
    wkv_pad[:, :48] = k_w[...]
    wkv_pad[:, VOFF : VOFF + 48] = v_w[...]
    wo_pad[VOFF : VOFF + 48, :] = o_w[...]

    @pl.loop(0, BR)
    def _(r):
        part = pl.ds(pl.multiple_of(r * BLK, BLK), BLK)
        normed = layer_norm(nodes[part, :].astype(F32))[0].astype(BF16)
        queries[r] = dot_nn(normed, wq_pad[...]).astype(BF16)
        kv_own[r] = dot_nn(normed, wkv_pad[...]).astype(BF16)
        cots[r] = dot_nt(cotan[part, :], wo_pad[...]).astype(BF16)

    for n in range(14):
        kv_s[n] = kv_own[kvstage[n]]
    gpeers = [grp_peer(grp, offset) for offset in GRP_ORDER]
    kv_c = [
        to_grp(kv_s.at[pl.ds((o - 1) * 2, 2)], kv_r.at[pl.ds((o - 1) * 2, 2)], kv_ss.at[n], kv_rs.at[n], gpeers[n])
        for n, o in enumerate(GRP_ORDER)
    ]
    for c in kv_c:
        c.start()

    x_c = []
    for q in range(QC):
        own_c[q].wait()
        for c in right_c[q]:
            c.wait()

        @pl.loop(0, 56)
        def _(n):
            xs[q][n] = right[q][stage[n]]

        x_c.append([
            to_grp(xs[q].at[pl.ds((o - 1) * 8, 8)], xr[q].at[pl.ds((o - 1) * 8, 8)], x_ss.at[q, n], x_rs.at[q, n], gpeers[n])
            for n, o in enumerate(GRP_ORDER)
        ])
        for c in x_c[q]:
            c.start()

    for c in kv_c:
        c.wait()
    own_c[2 * QC].wait()
    for c in bias_c:
        c.wait()
    kv_all[:BR] = kv_own[...]
    kv_all[BR:] = kv_r[...]
    chain_bias = same[row]

    @pl.loop(0, BR)
    def _(r):
        here = chain[grp * BR + r]
        query = queries[r]
        cot = cots[r]
        top = jnp.full((BLK, 1), -jnp.inf, F32)
        for s in range(KS):
            kv = kv_all[kvplace[r * KS + s]]
            j = cols[grp * BR + r, s]
            extra = jnp.where(chain[j] == here, chain_bias, 0.0)
            part = dot_nt(query, kv) * (48 ** -0.5) + (bias[r * KS + s].astype(F32) + extra)
            part = jnp.where(mask[grp * BR + r, s] > 0, part, -jnp.inf)
            scores[s] = part
            gprobs[s] = dot_nt(cot, kv)
            top = jnp.maximum(top, jnp.max(part, axis=1, keepdims=True))
        total = jnp.zeros((BLK, 1), F32)
        for s in range(KS):
            part = jnp.exp(scores[s] - top)
            scores[s] = part
            total = total + jnp.sum(part, axis=1, keepdims=True)
        inverse = 1.0 / total
        dots = jnp.zeros((BLK, 1), F32)
        mix = jnp.zeros((BLK, PAD), F32)
        for s in range(KS):
            probs = scores[s] * inverse
            scores[s] = probs
            dots = dots + jnp.sum(probs * gprobs[s], axis=1, keepdims=True)
            mix = mix + dot_nn(probs.astype(BF16), kv_all[kvplace[r * KS + s]])
        for s in range(KS):
            grads[r * KS + s] = (scores[s] * (gprobs[s] - dots)).astype(BF16)
        mixed[pl.ds(pl.multiple_of(r * BLK, BLK), BLK), :] = mix.astype(BF16)

    slot = lambda p: pl.ds(pl.multiple_of(p * 8, 8), 8)
    rows32 = lambda p: pl.ds(pl.multiple_of(p * 32, 32), 32)
    mix_c = [
        to_row(mixed.at[rows32(p)], mixed_r.at[row], mix_ss.at[n], mix_rs.at[n], p) for n, p in enumerate(peers)
    ]
    mix_own = pltpu.make_async_copy(mixed.at[rows32(row)], mixed_r.at[row], own_s.at[2 * QC + 2])
    grad_c = [
        to_row(grads.at[:, slot(p), :], grad_out.at[row], grad_ss.at[n], grad_rs.at[n], p)
        for n, p in enumerate(peers)
    ]
    grad_own = pltpu.make_async_copy(grads.at[:, mine, :], grad_out.at[row], own_s.at[2 * QC + 3])
    for c in mix_c + [mix_own] + grad_c + [grad_own]:
        c.start()

    tri_c, tri_own = [], []
    for q in range(QC):
        own_c[QC + q].wait()
        for c in left_c[q]:
            c.wait()
        for c in x_c[q]:
            c.wait()

        @pl.loop(0, NB)
        def _(b):
            r = b // KS
            lhs, rhs = [], []
            for t in range(KS):
                code = place[b * KS + t]
                near = right[q][jnp.minimum(code, NB - 1)]
                far = xr[q][jnp.clip(code - NB, 0, 55)]
                block = jnp.where(code < NB, near, far)
                rhs.append(jnp.where(code < NB + 56, block, jnp.zeros_like(block)))
                lhs.append(left[q][r * KS + t])
            tri[q][b] = dot_nt(jnp.concatenate(lhs, axis=1), jnp.concatenate(rhs, axis=1)).astype(BF16)

        tri_c.append([
            to_row(tri[q].at[:, slot(p), :], tri_out.at[q, row], tri_ss.at[q, n], tri_rs.at[q, n], p)
            for n, p in enumerate(peers)
        ])
        tri_own.append(pltpu.make_async_copy(tri[q].at[:, mine, :], tri_out.at[q, row], own_s.at[2 * QC + 4 + q]))
        for c in tri_c[q] + [tri_own[q]]:
            c.start()

    own_c[2 * QC + 1].wait()
    for c in wo_c + mix_c + [mix_own]:
        c.wait()
    acc = nodes[rows32(row), :].astype(F32)
    for p in range(ROW):
        acc = acc + dot_nn(mixed_r[p], wo_all[p])
    node_out[...] = acc.astype(BF16)

    for c in grad_c + [grad_own]:
        c.wait()
    for q in range(QC):
        for c in tri_c[q] + [tri_own[q]]:
            c.wait()


def exchange(scalars, tensors, nodes):
    smem = pl.BlockSpec(memory_space=pltpu.SMEM)
    vmem = pl.BlockSpec(memory_space=pltpu.VMEM)
    anyspace = pl.BlockSpec(memory_space=pl.ANY)
    dma = pltpu.SemaphoreType.DMA
    blocks = lambda n: pltpu.VMEM((n, BLK, BLK), BF16)
    n = ROW - 1
    scratch = (
        [blocks(NB)] * QC + [blocks(NB)] * QC + [blocks(NB)] * QC + [blocks(56)] * QC + [blocks(56)] * QC
        + [
            blocks(NB), blocks(NB), blocks(BR), blocks(14), blocks(14), blocks(BR + 14), blocks(BR), blocks(BR),
            pltpu.VMEM((BR * BLK, PAD), BF16), pltpu.VMEM((ROW, 32, PAD), BF16),
            pltpu.VMEM((ROW, PAD, 768), BF16), pltpu.VMEM((768, PAD), BF16), pltpu.VMEM((768, PAD), BF16),
            pltpu.VMEM((PAD, 768), BF16), pltpu.VMEM((KS, BLK, BLK), F32), pltpu.VMEM((KS, BLK, BLK), F32),
        ]
        + [dma((QC, n))] * 6 + [dma((QC, 7))] * 2 + [dma((7,))] * 2 + [dma((n,))] * 8 + [dma((2 * QC + 4 + QC,))]
    )
    return pl.pallas_call(
        exchange_kernel,
        in_specs=[smem] * 8 + [anyspace] * 3 + [vmem] * 6,
        out_specs=[anyspace, anyspace, vmem],
        out_shape=[
            jax.ShapeDtypeStruct((QC, ROW, NB, 8, BLK), BF16),
            jax.ShapeDtypeStruct((ROW, NB, 8, BLK), BF16),
            jax.ShapeDtypeStruct((32, 768), BF16),
        ],
        scratch_shapes=scratch,
        compiler_params=pltpu.CompilerParams(
            collective_id=0, has_side_effects=True, vmem_limit_bytes=63 << 20
        ),
        name="exchange",
    )(*scalars, *tensors, *nodes)


def finish_kernel(pair, tri, grads, gate_w, out_w, bias_w, pair_out, pair_grad, weights, turned):
    @pl.when(pl.program_id(0) == 0)
    def _():
        weights[...] = jnp.zeros_like(weights)
        weights[:CH, :CZ] = out_w[...]
        weights[CH:, CZ:] = bias_w[...]

    sums = tri[:, 0].astype(F32)
    shifted = sums - jnp.mean(sums, axis=0, keepdims=True)
    spread = jnp.mean(shifted * shifted, axis=0, keepdims=True)
    turned[: 8 * CH] = (shifted * lax.rsqrt(spread + EPS)).reshape(8 * CH, BLK)
    turned[8 * CH :] = grads[:, 0].astype(F32).reshape(8 * ROW, BLK)
    for i in range(8):
        hidden = turned[pl.ds(i, CH + ROW, stride=8), :].astype(BF16)
        both = dot_tn(hidden, weights[...])
        feats = pair[0, i].astype(F32)
        normed, scale = layer_norm(feats)
        gate = jax.nn.sigmoid(dot_nn(normed.astype(BF16), gate_w[...])).astype(BF16).astype(F32)
        pair_out[0, i] = (feats + gate * both[:, :CZ]).astype(BF16)
        grad = both[:, CZ:]
        centred = grad - jnp.mean(grad, axis=-1, keepdims=True)
        along = jnp.mean(grad * normed, axis=-1, keepdims=True)
        pair_grad[0, i] = (scale * (centred - normed * along)).astype(BF16)


def finish(pair, tri, grads, gate_w, out_w, bias_w):
    by_block = lambda n: pl.BlockSpec((n, 1, 8, BLK), lambda b: (0, b, 0, 0))
    whole = lambda a: pl.BlockSpec(a.shape, lambda b: (0,) * a.ndim)
    pair_spec = pl.BlockSpec((1, 8, BLK, CZ), lambda b: (b, 0, 0, 0))
    return pl.pallas_call(
        finish_kernel,
        grid=(NB,),
        in_specs=[pair_spec, by_block(CH), by_block(ROW), whole(gate_w), whole(out_w), whole(bias_w)],
        out_specs=[pair_spec, pair_spec],
        out_shape=[jax.ShapeDtypeStruct(pair.shape, BF16)] * 2,
        scratch_shapes=[
            pltpu.VMEM((CH + ROW, 2 * CZ), BF16),
            pltpu.VMEM(((CH + ROW) * 8, BLK), F32),
        ],
        compiler_params=pltpu.CompilerParams(vmem_limit_bytes=40 << 20),
        name="finish",
    )(pair, tri, grads, gate_w, out_w, bias_w)


def per_device(
    pair_feats,
    block_cols,
    attn_mask,
    chain_of_row,
    same_chain,
    node_feats,
    node_cotangent,
    tri_weight,
    gate_weight,
    tri_out_weight,
    bias_weight,
    query_weight,
    key_weight,
    value_weight,
    out_weight,
):
    pair = pair_feats.reshape(NB, 8, BLK, CZ)
    bias_t = bias_weight.T
    left, right, bias, place, kvplace, stage, kvstage = project(block_cols, pair, tri_weight, bias_t)
    tri, grads, node_out = exchange(
        (block_cols, attn_mask, chain_of_row, same_chain, place, kvplace, stage, kvstage),
        (left, right, bias),
        (node_feats, node_cotangent, query_weight, key_weight, value_weight, out_weight),
    )
    pair_out, pair_grad = finish(
        pair, tri.reshape(CH, NB, 8, BLK), grads, gate_weight, tri_out_weight, bias_t
    )
    return pair_out.reshape(pair_feats.shape), node_out, pair_grad.reshape(pair_feats.shape)


def solution(mesh):
    pair_spec = P("grp", None, "row", None, None)
    node_spec = P("grp", None)
    in_specs = (
        (pair_spec,) + (P(),) * 4 + (node_spec,) * 2 + (P(),) * 4 + (P(None, "row"),) * 3 + (P("row", None),)
    )
    out_specs = (pair_spec, P(("grp", "row"), None), pair_spec)
    return jax.shard_map(per_device, mesh=mesh, in_specs=in_specs, out_specs=out_specs, check_vma=False)
```

time: 670 us -> 231 us (0.34); the launches traced: 657 us -> 231 us
  waiting for transfers between devices: 267 us -> 0 us
  Pallas kernels: 0 us -> 206 us
  local copies, waits for them, and re-layouts: 125 us -> 24.5 us
  matrix products: 98.7 us -> 0 us
  other arithmetic: 77.1 us -> 0 us
  starting transfers between devices: 46.8 us -> 0 us
  blocking collectives: 27.9 us -> 0 us
  between operations: 14.9 us -> 0.7 us
    all_to_all x7 -> x0, waiting for transfers between devices: 267 us -> none  [the longest x1 134 us: per_device(): lax.all_to_all(outgoing, 'grp', split_axis=0, concat_axis=0, tiled=True)]
    pallas_call x0 -> x3, Pallas kernels: none -> 206 us  [the longest x1 151 us: exchange(): pl.pallas_call(exchange_kernel, in_specs=[smem] * 8 + [anyspace] * 3 + [v...]
    dot_general x16 -> x0, matrix products: 98.7 us -> none  [the longest x1 23.4 us: triangle_row(): jnp.einsum('stu,sudjk->stdjk', matches, far_rows, preferred_element_type=...]
    all_to_all x7 -> x0, starting transfers between devices: 46.7 us -> none  [the longest x1 8.59 us: per_device(): lax.all_to_all(bias_rows, 'row', split_axis=2, concat_axis=3, tiled=True)]
    dot_general x2 -> x0, local copies, waits for them, and re-layouts: 37.3 us -> none  [the longest x1 24.7 us: per_device(): jnp.einsum('rsijc,cx->rsxij', normed_short, tri_weight, preferred_element...]
    all_to_all x3 -> x0, local copies, waits for them, and re-layouts: 37 us -> none  [the longest x1 24.9 us: per_device(): lax.all_to_all(outgoing, 'grp', split_axis=0, concat_axis=0, tiled=True)]
    convert_element_type x8 -> x0, other arithmetic: 35.9 us -> none  [the longest x1 18.2 us: per_device(): (pair_scale * (centre_grad - normed * projection_mean)).astype(jnp.bfloat16)]
    reduce_sum x8 -> x0, other arithmetic: 31.8 us -> none  [the longest x1 13.3 us: per_device(): projection_mean = jnp.mean(grad_normed * normed, axis=4, keepdims=True)]
  transfers between devices with their start and end apart: 8 -> 0, of which waited for: 3 -> 0; matrix products, arithmetic and copies ran while one was open for 39% -> 0% of each run, Pallas kernels for 0% -> 0%
where the time goes in v1:
time: 231 us
  Pallas kernels  206 us (89%)
  local copies, waits for them, and re-layouts  24.5 us (11%)
    pallas_call x1, Pallas kernels, exchange(): pl.pallas_call(exchange_kernel, in_specs=[smem] * 8 + [anyspace] * 3 + [v...  151 us
    pallas_call x1, Pallas kernels, finish(): pl.pallas_call(finish_kernel, grid=(NB,), in_specs=[pair_spec, by_block(C...  29.6 us
    pallas_call x1, Pallas kernels, project(): pl.pallas_call(project_kernel, grid=(NB,), in_specs=[smem, pl.BlockSpec((...  25 us
    unnamed x42, local copies, waits for them, and re-layouts  24.5 us

profile of v1, /device:TPU:1, one launch (start us, length us, event | category | flops | bytes accessed | tf_op | source)
XLA Modules:
  0.0 230.8 jit_solution(12751094533606968419)
XLA Ops:
  0.6 0.8 copy.19.cols.refs_0_
  1.4 1.4 copy.20.refs_1_
  2.8 1.7 copy.21.refs_13_
  4.5 1.7 copy.22.refs_14_
  6.2 1.7 copy.23.refs_15_
  7.9 2.8 %copy-done = bf16[4,6,8,128,128]{4,3,2,1,0:T(8,128)(2,1)S(1)} copy-done((bf16[4,6,8,128,128]{4,3,2,1,0:T(8,128)(2,1)S(1)}, bf16[4,6,8,128,128]{4,3,2,1,0:T(8,128)(2,1)}, u32[]{:S(2)}) %copy-start) | copy-done | bytes 6291480
  10.7 0.8 copy-done.8
  11.5 0.7 copy-done.11
  12.2 25.0 %project.1 = (bf16[64,24,8,128]{3,2,1,0:T(8,128)(2,1)S(1)}, bf16[64,24,8,128]{3,2,1,0:T(8,128)(2,1)S(1)}, bf16[16,24,8,128]{3,2,1,0:T(8,128)(2,1)S(1)}, s32[144]...) custom-call(s32[32,6]{1,0:T(8,128)S(1)} %copy.19.cols.refs_0_, bf16[24,8,128,128]{3,2,1,0:T(8,128)(2,1)S(1)} %bitcast.5, ...), custom_call_target="tpu_custom_call" | custom-call | tf_op jit(solution)/shard_map/project/pallas_call | solution.py:154
  37.2 0.0 copy-start.3
  37.2 1.7 copy-done.3
  38.9 1.7 copy-done.4
  40.5 0.9 copy-done.6
  41.4 0.6 copy-done.13
  42.0 0.5 copy-done.14
  42.5 0.5 copy-done.15
  43.1 0.6 copy-done.16
  43.7 151.0 %exchange.1 = (bf16[4,16,24,8,128]{4,3,2,1,0:T(8,128)(2,1)}, bf16[16,24,8,128]{3,2,1,0:T(8,128)(2,1)}, bf16[32,768]{1,0:T(8,128)(2,1)}) custom-call(s32[32,6]{1,0:T(8,128)} %copy-done.7, s32[32,6]{1,0:T(8,128)} %copy.20.refs_1_, s32[32]{0:T(128)} %refs_2_.1, f32[16]{0:T(128)} %refs_3_.1, s32[144]{0:T(256)} %copy-done.13, s32[24]{0:T(128)} %copy-done.14, ...), custom_call_target="tpu_custom_call" | custom-call | tf_op jit(solution)/shard_map/exchange/pallas_call | solution.py:427
  194.7 0.0 copy-start.1
  194.7 2.8 %copy-done.1 = bf16[4,6,8,128,128]{4,3,2,1,0:T(8,128)(2,1)S(1)} copy-done((bf16[4,6,8,128,128]{4,3,2,1,0:T(8,128)(2,1)S(1)}, bf16[4,6,8,128,128]{4,3,2,1,0:T(8,128)(2,1)}, u32[]{:S(2)}) %copy-start.1) | copy-done | bytes 6291480
  197.5 1.9 copy-done.2
  199.4 1.1 copy-done.5
  200.5 29.6 %finish.1 = (bf16[24,8,128,128]{3,2,1,0:T(8,128)(2,1)}, bf16[24,8,128,128]{3,2,1,0:T(8,128)(2,1)}) custom-call(bf16[24,8,128,128]{3,2,1,0:T(8,128)(2,1)S(1)} %bitcast.6, bf16[64,24,8,128]{3,2,1,0:T(8,128)(2,1)S(1)} %bitcast.7, bf16[16,24,8,128]{3,2,1,0:T(8,128)(2,1)S(1)} %copy-done.5, bf16[128,128]{1,0:T(8,128)(2,1)S(1)} %copy-done.9, ...), custom_call_target="tpu_custom_call" | custom-call | tf_op jit(solution)/shard_map/finish/pallas_call | solution.py:473
  230.1 0.6 copy.25
  (21 shorter events, 0.0 us)
Async XLA Ops:
  1.4 42.3 %copy-start.7 = (s32[32,6]{1,0:T(8,128)}, s32[32,6]{1,0:T(8,128)S(1)}, u32[]{:S(2)}) copy-start(s32[32,6]{1,0:T(8,128)S(1)} %copy.19.cols.refs_0_) | copy-start | bytes 2308
  7.9 2.8 %copy-start = (bf16[4,6,8,128,128]{4,3,2,1,0:T(8,128)(2,1)S(1)}, bf16[4,6,8,128,128]{4,3,2,1,0:T(8,128)(2,1)}, u32[]{:S(2)}) copy-start(bf16[4,6,8,128,128]{4,3,2,1,0:T(8,128)(2,1)} %param.15) | copy-start | bytes 18874372
  10.7 0.8 copy-start.8
  11.5 0.7 copy-start.11
  12.2 182.4 %copy-start.9 = (bf16[128,128]{1,0:T(8,128)(2,1)S(1)}, bf16[128,128]{1,0:T(8,128)(2,1)}, u32[]{:S(2)}) copy-start(bf16[128,128]{1,0:T(8,128)(2,1)} %gate_w.1) | copy-start | bytes 98308
  12.2 182.5 %copy-start.10 = (bf16[64,128]{1,0:T(8,128)(2,1)S(1)}, bf16[64,128]{1,0:T(8,128)(2,1)}, u32[]{:S(2)}) copy-start(bf16[64,128]{1,0:T(8,128)(2,1)} %out_w.1) | copy-start | bytes 49156
  12.2 182.5 %copy-start.12 = (bf16[128,16]{0,1:T(8,128)(2,1)S(1)}, bf16[128,16]{0,1:T(8,128)(2,1)}, u32[]{:S(2)}) copy-start(bf16[128,16]{0,1:T(8,128)(2,1)} %param.25) | copy-start | bytes 12292
  37.2 1.7 copy-start.3
  38.9 1.7 copy-start.4
  40.5 0.9 copy-start.6
  41.4 0.6 copy-start.13
  42.0 0.5 copy-start.14
  42.5 0.5 copy-start.15
  43.1 0.6 copy-start.16
  194.7 2.8 %copy-start.1 = (bf16[4,6,8,128,128]{4,3,2,1,0:T(8,128)(2,1)S(1)}, bf16[4,6,8,128,128]{4,3,2,1,0:T(8,128)(2,1)}, u32[]{:S(2)}) copy-start(bf16[4,6,8,128,128]{4,3,2,1,0:T(8,128)(2,1)} %param.15) | copy-start | bytes 18874372
  197.5 1.9 copy-start.2
  199.4 1.1 copy-start.5
  200.5 29.6 %copy-start.17 = (bf16[32,768]{1,0:T(8,128)(2,1)S(1)}, bf16[32,768]{1,0:T(8,128)(2,1)}, u32[]{:S(2)}) copy-start(bf16[32,768]{1,0:T(8,128)(2,1)} %get-tuple-element.31) | copy-start | bytes 147460

commit v2 on v1

v2 whole, which is shorter than its diff:
```python
import jax
import jax.numpy as jnp
from jax import lax
from jax.experimental import pallas as pl
from jax.experimental.pallas import tpu as pltpu
from jax.sharding import PartitionSpec as P

F32 = jnp.float32
BF16 = jnp.bfloat16
MESH = pl.DeviceIdType.MESH
EPS = 1e-5
GRP, ROW = 8, 16
BR, KS, BLK, CZ, CH = 4, 6, 128, 128, 64
NB = BR * KS
QC = CH // ROW
PAD = 128
VOFF = 64
HALVES = ((0, 6), (6, 18))
ROW_ORDER = (1, 3, 4, 12, 2, 8, 5, 15, 7, 13, 6, 14, 9, 11, 10)
GRP_ORDER = (2, 6, 4, 3, 7, 5, 1)


def row_peer(row, offset):
    z, y = row // 4, row % 4
    return ((z + offset // 4) % 4) * 4 + (y + offset % 4) % 4


def grp_peer(grp, offset):
    x, core = grp // 2, grp % 2
    return ((x + offset // 2) % 4) * 2 + (core + offset % 2) % 2


def shift_and_scale(values, ones, shifted, inverse):
    inverse[...] = dot_nn(values, ones)
    shifted[...] = values.astype(F32) - inverse[...]
    inverse[...] = dot_nn((shifted[...] * shifted[...]).astype(BF16), ones)
    inverse[...] = lax.rsqrt(inverse[...] + EPS)


def layer_norm(values):
    center = jnp.mean(values, axis=-1, keepdims=True)
    shifted = values - center
    spread = jnp.mean(shifted * shifted, axis=-1, keepdims=True)
    inverse = lax.rsqrt(spread + EPS)
    return shifted * inverse, inverse


def dot_nt(a, b):
    return lax.dot_general(a, b, (((1,), (1,)), ((), ())), preferred_element_type=F32)


def dot_nn(a, b):
    return lax.dot_general(a, b, (((1,), (0,)), ((), ())), preferred_element_type=F32)


def dot_tn(a, b):
    return lax.dot_general(a, b, (((0,), (0,)), ((), ())), preferred_element_type=F32)


def i32(flag):
    return jnp.where(flag, 1, 0).astype(jnp.int32)


def named_ranks(cols, reader, owner):
    flags = [jnp.int32(0)] * BR
    for r in range(BR):
        for s in range(KS):
            c = cols[s, reader * BR + r]
            for l in range(BR):
                flags[l] = flags[l] | i32(c == owner * BR + l)
    ranks, count = [], jnp.int32(0)
    firsts = [jnp.int32(0), jnp.int32(0)]
    for l in range(BR):
        ranks.append(count)
        for a in range(2):
            firsts[a] = firsts[a] + l * flags[l] * i32(count == a)
        count = count + flags[l]
    return ranks, firsts


def pick(entries, index):
    out = jnp.int32(0)
    for n, entry in enumerate(entries):
        out = out + entry * i32(index == n)
    return out


def write_places(cols, grp, step, place, kvplace):
    inner = step // KS
    slot = step % KS
    j = cols[slot, grp * BR + inner]
    owner = j >> 2
    own = owner == grp
    ranks, _ = named_ranks(cols, grp, owner)
    offset = ((grp // 2 - owner // 2 + 4) % 4) * 2 + (grp % 2 - owner % 2 + 2) % 2
    rank_j = pick(ranks, j & 3)
    theirs = [cols[u, j] for u in range(KS)]
    for t in range(KS):
        c = cols[t, grp * BR + inner]
        found, far, count = jnp.int32(-1), jnp.int32(0), jnp.int32(0)
        for u in range(KS):
            hit = theirs[u] == c
            found = jnp.where(hit, u, found)
            far = jnp.where(hit, count, far)
            count = count + i32((theirs[u] >> 2) != owner)
        n = jnp.where((c >> 2) == owner, pick(ranks, c & 3), 2 + far)
        remote = NB + (offset - 1) * 8 + rank_j * 4 + n
        place[step * KS + t] = jnp.where(
            found >= 0, jnp.where(own, (j & 3) * KS + found, remote), NB + 56
        )
    kvplace[step] = jnp.where(own, j & 3, BR + (offset - 1) * 2 + rank_j)


def write_stages(cols, grp, to, stage, kvstage):
    reader = grp_peer(grp, to)
    _, firsts = named_ranks(cols, reader, grp)
    for a in range(2):
        near, far = [jnp.int32(0)] * 2, [jnp.int32(0)] * 2
        count = jnp.int32(0)
        for u in range(KS):
            c = cols[u, grp * BR + firsts[a]]
            away = i32((c >> 2) != grp)
            for n in range(2):
                near[n] = near[n] + u * i32(c == grp * BR + firsts[n])
                far[n] = far[n] + u * away * i32(count == n)
            count = count + away
        for n in range(2):
            stage[(to - 1) * 8 + a * 4 + n] = firsts[a] * KS + near[n]
            stage[(to - 1) * 8 + a * 4 + 2 + n] = firsts[a] * KS + far[n]
        kvstage[(to - 1) * 2 + a] = firsts[a]


def exchange_kernel(*refs):
    (
        cols, mask, chain, same, pair, tri_w, bias_w, nodes, cotan, q_w, k_w, v_w, o_w,
        tri_out, grad_out, node_out,
    ) = refs[:16]
    scr = list(refs[16:])
    take = lambda n: [scr.pop(0) for _ in range(n)]
    right = take(QC)
    left = take(QC)
    tri = take(QC)
    xs = take(QC)
    xr = take(QC)
    sources = [take(3) for _ in range(2)]
    pair_v = take(2)
    weights, ones, turned, shifted, inverse, normed_s, place, kvplace, stage, kvstage = take(10)
    (bias, grads, kv_own, kv_s, kv_r, kv_all, queries, cots, mixed, mixed_r, wo_all,
     wq_pad, wkv_pad, wo_pad, scores, gprobs) = take(16)
    (right_ss, right_rs, left_ss, left_rs, tri_ss, tri_rs, x_ss, x_rs,
     kv_ss, kv_rs, grad_ss, grad_rs, mix_ss, mix_rs, wo_ss, wo_rs, bias_ss, bias_rs, own_s, pair_s) = take(20)

    grp = lax.axis_index("grp")
    row = lax.axis_index("row")
    mine = pl.ds(pl.multiple_of(row * 8, 8), 8)

    def to_row(src, dst, ss, rs, peer):
        return pltpu.make_async_remote_copy(
            src, dst, ss, rs, device_id=(grp, peer), device_id_type=MESH
        )

    def to_grp(src, dst, ss, rs, peer):
        return pltpu.make_async_remote_copy(
            src, dst, ss, rs, device_id=(peer, row), device_id_type=MESH
        )

    loads = [
        pltpu.make_async_copy(pair.at[pl.ds(first, count)], pair_v[h], pair_s.at[h])
        for h, (first, count) in enumerate(HALVES)
    ]
    for c in loads:
        c.start()

    wo_all[...] = jnp.zeros_like(wo_all)
    wo_pad[...] = jnp.zeros_like(wo_pad)
    weights[: 4 * CH, :] = (tri_w[...].astype(F32).T * 0.5).astype(BF16)
    weights[4 * CH :, :] = bias_w[...]
    ones[...] = jnp.full_like(ones, 1.0 / CZ)

    barrier = pltpu.get_barrier_semaphore()
    for offset in ROW_ORDER:
        pl.semaphore_signal(barrier, inc=1, device_id=(grp, row_peer(row, offset)), device_id_type=MESH)
    for offset in GRP_ORDER:
        pl.semaphore_signal(barrier, inc=1, device_id=(grp_peer(grp, offset), row), device_id_type=MESH)
    pl.semaphore_wait(barrier, 22)

    peers = [row_peer(row, offset) for offset in ROW_ORDER]

    right_c = [[] for _ in range(QC)]
    left_c = [[] for _ in range(QC)]
    bias_c = []
    own_right, own_left, own_bias = [[] for _ in range(QC)], [[] for _ in range(QC)], []
    for h, (first, count) in enumerate(HALVES):
        left_s, right_s, bias_s = sources[h]
        here = pl.ds(first, count)
        for q in range(QC):
            right_c[q].append([
                to_row(right_s.at[q * ROW + p], right[q].at[here, mine, :], right_ss.at[h * QC + q, n], right_rs.at[h * QC + q, n], p)
                for n, p in enumerate(peers)
            ])
            left_c[q].append([
                to_row(left_s.at[q * ROW + p], left[q].at[here, mine, :], left_ss.at[h * QC + q, n], left_rs.at[h * QC + q, n], p)
                for n, p in enumerate(peers)
            ])
            own_right[q].append(pltpu.make_async_copy(right_s.at[q * ROW + row], right[q].at[here, mine, :], own_s.at[h, q]))
            own_left[q].append(pltpu.make_async_copy(left_s.at[q * ROW + row], left[q].at[here, mine, :], own_s.at[h, QC + q]))
        bias_c.append([
            to_row(bias_s.at[p], bias.at[here, mine, :], bias_ss.at[h, n], bias_rs.at[h, n], p)
            for n, p in enumerate(peers)
        ])
        own_bias.append(pltpu.make_async_copy(bias_s.at[row], bias.at[here, mine, :], own_s.at[h, 2 * QC]))
    wo_c = [
        to_row(o_w, wo_all.at[row, pl.ds(VOFF, 48), :], wo_ss.at[n], wo_rs.at[n], p)
        for n, p in enumerate(peers)
    ]
    wo_own = pltpu.make_async_copy(o_w, wo_all.at[row, pl.ds(VOFF, 48), :], own_s.at[0, 2 * QC + 1])

    for h, (first, count) in enumerate(HALVES):
        left_s, right_s, bias_s = sources[h]
        loads[h].wait()

        @pl.loop(0, count)
        def _(b):
            shift_and_scale(pair_v[h][b].reshape(8 * BLK, CZ), ones[...], shifted, inverse)
            normed_s[...] = (shifted[...] * inverse[...]).astype(BF16)
            for i in range(8):
                projected = dot_nt(weights[...], normed_s[i * BLK : (i + 1) * BLK, :])
                turned[pl.ds(i, CH, stride=8), :] = (jnp.tanh(projected[CH : 2 * CH]) + 1.0) * projected[:CH]
                turned[pl.ds(8 * CH + i, CH, stride=8), :] = (
                    jnp.tanh(projected[3 * CH : 4 * CH]) + 1.0
                ) * projected[2 * CH : 3 * CH]
                turned[pl.ds(16 * CH + i, ROW, stride=8), :] = projected[4 * CH :]
            left_s[:, b] = turned[: 8 * CH].reshape(CH, 8, BLK).astype(BF16)
            right_s[:, b] = turned[8 * CH : 16 * CH].reshape(CH, 8, BLK).astype(BF16)
            bias_s[:, b] = turned[16 * CH :].reshape(ROW, 8, BLK).astype(BF16)

        for q in range(QC):
            for c in right_c[q][h] + [own_right[q][h]]:
                c.start()
        if h == 0:
            for c in bias_c[0] + [own_bias[0]]:
                c.start()
    for q in range(QC):
        for c in left_c[q][0] + [own_left[q][0]]:
            c.start()
    for c in bias_c[1] + [own_bias[1]]:
        c.start()
    for q in range(QC):
        for c in left_c[q][1] + [own_left[q][1]]:
            c.start()
    for c in wo_c + [wo_own]:
        c.start()

    wq_pad[...] = jnp.zeros_like(wq_pad)
    wkv_pad[...] = jnp.zeros_like(wkv_pad)
    wq_pad[:48, :] = q_w[...]
    wkv_pad[:48, :] = k_w[...]
    wkv_pad[VOFF : VOFF + 48, :] = v_w[...]
    wo_pad[VOFF : VOFF + 48, :] = o_w[...]

    @pl.loop(0, BR)
    def _(r):
        part = pl.ds(pl.multiple_of(r * BLK, BLK), BLK)
        normed = layer_norm(nodes[part, :].astype(F32))[0].astype(BF16)
        queries[r] = dot_nt(normed, wq_pad[...]).astype(BF16)
        kv_own[r] = dot_nt(normed, wkv_pad[...]).astype(BF16)
        cots[r] = dot_nt(cotan[part, :], wo_pad[...]).astype(BF16)

    @pl.loop(1, GRP)
    def _(to):
        write_stages(cols, grp, to, stage, kvstage)

    for n in range(14):
        kv_s[n] = kv_own[kvstage[n]]
    gpeers = [grp_peer(grp, offset) for offset in GRP_ORDER]
    kv_c = [
        to_grp(kv_s.at[pl.ds((o - 1) * 2, 2)], kv_r.at[pl.ds((o - 1) * 2, 2)], kv_ss.at[n], kv_rs.at[n], gpeers[n])
        for n, o in enumerate(GRP_ORDER)
    ]
    for c in kv_c:
        c.start()

    x_c = []
    for q in range(QC):
        for h in range(2):
            for c in right_c[q][h] + [own_right[q][h]]:
                c.wait()

        @pl.loop(0, 56)
        def _(n):
            xs[q][n] = right[q][stage[n]]

        x_c.append([
            to_grp(xs[q].at[pl.ds((o - 1) * 8, 8)], xr[q].at[pl.ds((o - 1) * 8, 8)], x_ss.at[q, n], x_rs.at[q, n], gpeers[n])
            for n, o in enumerate(GRP_ORDER)
        ])
        for c in x_c[q]:
            c.start()

    @pl.loop(0, NB)
    def _(b):
        write_places(cols, grp, b, place, kvplace)

    for c in kv_c:
        c.wait()
    for h in range(2):
        for c in bias_c[h] + [own_bias[h]]:
            c.wait()
    kv_all[:BR] = kv_own[...]
    kv_all[BR:] = kv_r[...]
    chain_bias = same[row]

    @pl.loop(0, BR)
    def _(r):
        here = chain[grp * BR + r]
        query = queries[r]
        cot = cots[r]
        top = jnp.full((BLK, 1), -jnp.inf, F32)
        for s in range(KS):
            kv = kv_all[kvplace[r * KS + s]]
            j = cols[s, grp * BR + r]
            extra = jnp.where(chain[j] == here, chain_bias, 0.0)
            part = dot_nt(query, kv) * (48 ** -0.5) + (bias[r * KS + s].astype(F32) + extra)
            part = jnp.where(mask[s, grp * BR + r] > 0, part, -jnp.inf)
            scores[s] = part
            gprobs[s] = dot_nt(cot, kv)
            top = jnp.maximum(top, jnp.max(part, axis=1, keepdims=True))
        total = jnp.zeros((BLK, 1), F32)
        for s in range(KS):
            part = jnp.exp(scores[s] - top)
            scores[s] = part
            total = total + jnp.sum(part, axis=1, keepdims=True)
        inverse = 1.0 / total
        dots = jnp.zeros((BLK, 1), F32)
        mix = jnp.zeros((BLK, PAD), F32)
        for s in range(KS):
            probs = scores[s] * inverse
            scores[s] = probs
            dots = dots + jnp.sum(probs * gprobs[s], axis=1, keepdims=True)
            mix = mix + dot_nn(probs.astype(BF16), kv_all[kvplace[r * KS + s]])
        for s in range(KS):
            grads[r * KS + s] = (scores[s] * (gprobs[s] - dots)).astype(BF16)
        mixed[pl.ds(pl.multiple_of(r * BLK, BLK), BLK), :] = mix.astype(BF16)

    slot = lambda p: pl.ds(pl.multiple_of(p * 8, 8), 8)
    rows32 = lambda p: pl.ds(pl.multiple_of(p * 32, 32), 32)
    mix_c = [
        to_row(mixed.at[rows32(p)], mixed_r.at[row], mix_ss.at[n], mix_rs.at[n], p) for n, p in enumerate(peers)
    ]
    mix_own = pltpu.make_async_copy(mixed.at[rows32(row)], mixed_r.at[row], own_s.at[0, 2 * QC + 2])
    grad_c = [
        to_row(grads.at[:, slot(p), :], grad_out.at[row], grad_ss.at[n], grad_rs.at[n], p)
        for n, p in enumerate(peers)
    ]
    grad_own = pltpu.make_async_copy(grads.at[:, mine, :], grad_out.at[row], own_s.at[0, 2 * QC + 3])
    for c in mix_c + [mix_own] + grad_c + [grad_own]:
        c.start()

    tri_c, tri_own = [], []
    for q in range(QC):
        for h in range(2):
            for c in left_c[q][h] + [own_left[q][h]]:
                c.wait()
        for c in x_c[q]:
            c.wait()

        @pl.loop(0, NB)
        def _(b):
            r = b // KS
            lhs, rhs = [], []
            for t in range(KS):
                code = place[b * KS + t]
                near = right[q][jnp.minimum(code, NB - 1)]
                far = xr[q][jnp.clip(code - NB, 0, 55)]
                block = jnp.where(code < NB, near, far)
                rhs.append(jnp.where(code < NB + 56, block, jnp.zeros_like(block)))
                lhs.append(left[q][r * KS + t])
            tri[q][b] = dot_nt(jnp.concatenate(lhs, axis=1), jnp.concatenate(rhs, axis=1)).astype(BF16)

        tri_c.append([
            to_row(tri[q].at[:, slot(p), :], tri_out.at[q, row], tri_ss.at[q, n], tri_rs.at[q, n], p)
            for n, p in enumerate(peers)
        ])
        tri_own.append(pltpu.make_async_copy(tri[q].at[:, mine, :], tri_out.at[q, row], own_s.at[1, 2 * QC + 1 + q]))
        for c in tri_c[q] + [tri_own[q]]:
            c.start()

    for c in wo_c + [wo_own] + mix_c + [mix_own]:
        c.wait()
    acc = nodes[rows32(row), :].astype(F32)
    for p in range(ROW):
        acc = acc + dot_nn(mixed_r[p], wo_all[p])
    node_out[...] = acc.astype(BF16)

    for c in grad_c + [grad_own]:
        c.wait()
    for q in range(QC):
        for c in tri_c[q] + [tri_own[q]]:
            c.wait()


def exchange(scalars, tensors, nodes):
    smem = pl.BlockSpec(memory_space=pltpu.SMEM)
    vmem = pl.BlockSpec(memory_space=pltpu.VMEM)
    anyspace = pl.BlockSpec(memory_space=pl.ANY)
    dma = pltpu.SemaphoreType.DMA
    blocks = lambda n: pltpu.VMEM((n, BLK, BLK), BF16)
    blocks_2d = pltpu.VMEM((BLK, BLK), BF16)
    n = ROW - 1
    scratch = (
        [blocks(NB)] * QC + [blocks(NB)] * QC + [blocks(NB)] * QC + [blocks(56)] * QC + [blocks(56)] * QC
        + [pltpu.VMEM((c, k, 8, BLK), BF16) for _, k in HALVES for c in (CH, CH, ROW)]
        + [pltpu.VMEM((k, 8, BLK, CZ), BF16) for _, k in HALVES]
        + [
            pltpu.VMEM((4 * CH + ROW, CZ), BF16), blocks_2d, pltpu.VMEM(((2 * CH + ROW) * 8, BLK), F32),
            pltpu.VMEM((8 * BLK, CZ), F32), pltpu.VMEM((8 * BLK, CZ), F32), pltpu.VMEM((8 * BLK, CZ), BF16),
            pltpu.SMEM((NB * KS,), jnp.int32), pltpu.SMEM((NB,), jnp.int32),
            pltpu.SMEM((56,), jnp.int32), pltpu.SMEM((14,), jnp.int32),
        ]
        + [
            blocks(NB), blocks(NB), blocks(BR), blocks(14), blocks(14), blocks(BR + 14), blocks(BR), blocks(BR),
            pltpu.VMEM((BR * BLK, PAD), BF16), pltpu.VMEM((ROW, 32, PAD), BF16),
            pltpu.VMEM((ROW, PAD, 768), BF16), pltpu.VMEM((PAD, 768), BF16), pltpu.VMEM((PAD, 768), BF16),
            pltpu.VMEM((PAD, 768), BF16), pltpu.VMEM((KS, BLK, BLK), F32), pltpu.VMEM((KS, BLK, BLK), F32),
        ]
        + [dma((2 * QC, n))] * 4 + [dma((QC, n))] * 2 + [dma((QC, 7))] * 2 + [dma((7,))] * 2 + [dma((n,))] * 6 + [dma((2, n))] * 2
        + [dma((2, 2 * QC + 1 + QC)), dma((2,))]
    )
    return pl.pallas_call(
        exchange_kernel,
        in_specs=[smem] * 4 + [anyspace] + [vmem] * 8,
        out_specs=[anyspace, anyspace, vmem],
        out_shape=[
            jax.ShapeDtypeStruct((QC, ROW, NB, 8, BLK), BF16),
            jax.ShapeDtypeStruct((ROW, NB, 8, BLK), BF16),
            jax.ShapeDtypeStruct((32, 768), BF16),
        ],
        scratch_shapes=scratch,
        compiler_params=pltpu.CompilerParams(
            collective_id=0, has_side_effects=True, vmem_limit_bytes=63 << 20
        ),
        name="exchange",
    )(*scalars, *tensors, *nodes)


def finish_kernel(
    pair, tri, grads, gate_w, out_w, bias_w, pair_out, pair_grad,
    weights, gates, ones, turned, shifted, inverse, hidden, gate, both,
):
    @pl.when(pl.program_id(0) == 0)
    def _():
        bias = bias_w[...].astype(F32)
        weights[...] = jnp.zeros_like(weights)
        weights[:CH, :CZ] = out_w[...] * 0.5
        weights[CH : CH + ROW, CZ:] = (bias - jnp.mean(bias, axis=1, keepdims=True)).astype(BF16)
        gates[...] = gate_w[...] * 0.5
        ones[...] = jnp.full_like(ones, 1.0 / CZ)
        turned[...] = jnp.zeros_like(turned)

    feats = pair[0].reshape(8 * BLK, CZ)
    shift_and_scale(feats, ones[...], shifted, inverse)
    shifted[...] = shifted[...] * inverse[...]
    gate[...] = dot_nn(shifted[...].astype(BF16), gates[...])

    sums = tri[:, 0].astype(F32)
    centred = sums - jnp.mean(sums, axis=0, keepdims=True)
    spread = jnp.mean(centred * centred, axis=0, keepdims=True)
    turned[: 8 * CH] = (centred * lax.rsqrt(spread + EPS)).reshape(8 * CH, BLK)
    turned[8 * CH : 8 * (CH + ROW)] = grads[:, 0].astype(F32).reshape(8 * ROW, BLK)
    for i in range(8):
        hidden[i * BLK : (i + 1) * BLK, :] = turned[pl.ds(i, PAD, stride=8), :].astype(BF16).T
    both[...] = dot_nn(hidden[...], weights[...])

    pair_out[0] = (
        (feats.astype(F32) + (jnp.tanh(gate[...]) + 1.0) * both[:, :CZ]).astype(BF16).reshape(8, BLK, CZ)
    )
    gate[...] = dot_nn((both[:, CZ:] * shifted[...]).astype(BF16), ones[...])
    pair_grad[0] = (
        (inverse[...] * (both[:, CZ:] - shifted[...] * gate[...])).astype(BF16).reshape(8, BLK, CZ)
    )


def finish(pair, tri, grads, gate_w, out_w, bias_w):
    by_block = lambda n: pl.BlockSpec((n, 1, 8, BLK), lambda b: (0, b, 0, 0))
    whole = lambda a: pl.BlockSpec(a.shape, lambda b: (0,) * a.ndim)
    pair_spec = pl.BlockSpec((1, 8, BLK, CZ), lambda b: (b, 0, 0, 0))
    return pl.pallas_call(
        finish_kernel,
        grid=(NB,),
        in_specs=[pair_spec, by_block(CH), by_block(ROW), whole(gate_w), whole(out_w), whole(bias_w)],
        out_specs=[pair_spec, pair_spec],
        out_shape=[jax.ShapeDtypeStruct(pair.shape, BF16)] * 2,
        scratch_shapes=[
            pltpu.VMEM((PAD, 2 * CZ), BF16),
            pltpu.VMEM((CZ, CZ), BF16),
            pltpu.VMEM((CZ, CZ), BF16),
            pltpu.VMEM((PAD * 8, BLK), F32),
            pltpu.VMEM((8 * BLK, CZ), F32),
            pltpu.VMEM((8 * BLK, CZ), F32),
            pltpu.VMEM((8 * BLK, PAD), BF16),
            pltpu.VMEM((8 * BLK, CZ), F32),
            pltpu.VMEM((8 * BLK, 2 * CZ), F32),
        ],
        compiler_params=pltpu.CompilerParams(vmem_limit_bytes=62 << 20),
        name="finish",
    )(pair, tri, grads, gate_w, out_w, bias_w)


def per_device(
    pair_feats,
    block_cols,
    attn_mask,
    chain_of_row,
    same_chain,
    node_feats,
    node_cotangent,
    tri_weight,
    gate_weight,
    tri_out_weight,
    bias_weight,
    query_weight,
    key_weight,
    value_weight,
    out_weight,
):
    pair = pair_feats.reshape(NB, 8, BLK, CZ)
    bias_t = bias_weight.T
    tri, grads, node_out = exchange(
        (block_cols.T, attn_mask.T, chain_of_row, same_chain),
        (pair, tri_weight, bias_t),
        (node_feats, node_cotangent, query_weight.T, key_weight.T, value_weight.T, out_weight),
    )
    pair_out, pair_grad = finish(
        pair, tri.reshape(CH, NB, 8, BLK), grads, gate_weight, tri_out_weight, bias_t
    )
    return pair_out.reshape(pair_feats.shape), node_out, pair_grad.reshape(pair_feats.shape)


def solution(mesh):
    pair_spec = P("grp", None, "row", None, None)
    node_spec = P("grp", None)
    in_specs = (
        (pair_spec,) + (P(),) * 4 + (node_spec,) * 2 + (P(),) * 4 + (P(None, "row"),) * 3 + (P("row", None),)
    )
    out_specs = (pair_spec, P(("grp", "row"), None), pair_spec)
    return jax.shard_map(per_device, mesh=mesh, in_specs=in_specs, out_specs=out_specs, check_vma=False)
```

time: 231 us -> 189 us (0.82)
  local copies, waits for them, and re-layouts: 24.5 us -> 0.62 us
  Pallas kernels: 206 us -> 187 us
    unnamed x42 -> x3, local copies, waits for them, and re-layouts: 24.5 us -> 0.62 us
    pallas_call x2 -> x1, Pallas kernels: 176 us -> 162 us  [exchange(): pl.pallas_call(exchange_kernel, in_specs=[smem] * 4 + [anyspace] + [vmem]...]
    pallas_call x1, Pallas kernels: 29.6 us -> 25.2 us  [finish(): pl.pallas_call(finish_kernel, grid=(NB,), in_specs=[pair_spec, by_block(C...]
where the time goes in v2:
time: 189 us
  Pallas kernels  187 us (99%)
    pallas_call x1, Pallas kernels, exchange(): pl.pallas_call(exchange_kernel, in_specs=[smem] * 4 + [anyspace] + [vmem]...  162 us
    pallas_call x1, Pallas kernels, finish(): pl.pallas_call(finish_kernel, grid=(NB,), in_specs=[pair_spec, by_block(C...  25.2 us

profile of v2, /device:TPU:1, one launch (start us, length us, event | category | flops | bytes accessed | tf_op | source)
XLA Modules:
  0.0 188.5 jit_solution(2955831232569209706)
XLA Ops:
  0.6 162.0 %exchange.1 = (bf16[4,16,24,8,128]{4,3,2,1,0:T(8,128)(2,1)}, bf16[16,24,8,128]{3,2,1,0:T(8,128)(2,1)}, bf16[32,768]{1,0:T(8,128)(2,1)}) custom-call(s32[6,32]{1,0:T(8,128)} %bitcast.18, s32[6,32]{1,0:T(8,128)} %bitcast.19, s32[32]{0:T(128)} %refs_2_.1, f32[16]{0:T(128)} %refs_3_.1, bf16[24,8,128,128]{3,2,1,0:T(8,128)(2,1)} %bitcast.10, ...), custom_call_target="tpu_custom_call" | custom-call | tf_op jit(solution)/shard_map/exchange/pallas_call | solution.py:429
  162.7 0.0 copy-start
  162.7 25.2 %finish.1 = (bf16[24,8,128,128]{3,2,1,0:T(8,128)(2,1)}, bf16[24,8,128,128]{3,2,1,0:T(8,128)(2,1)}) custom-call(bf16[24,8,128,128]{3,2,1,0:T(8,128)(2,1)} %bitcast.11, bf16[64,24,8,128]{3,2,1,0:T(8,128)(2,1)} %bitcast.12, bf16[16,24,8,128]{3,2,1,0:T(8,128)(2,1)} %get-tuple-element.9.grads, bf16[128,128]{1,0:T(8,128)(2,1)} %gate_w.1, bf16[64,128]{1,0:T(8,128)(2,1)} %out_w.1, ...), custom_call_target="tpu_custom_call" | custom-call | tf_op jit(solution)/shard_map/finish/pallas_call | solution.py:487
  187.9 0.0 copy-done
  187.9 0.6 copy.19
Async XLA Ops:
  162.7 25.2 %copy-start = (bf16[32,768]{1,0:T(8,128)(2,1)S(1)}, bf16[32,768]{1,0:T(8,128)(2,1)}, u32[]{:S(2)}) copy-start(bf16[32,768]{1,0:T(8,128)(2,1)} %get-tuple-element.17) | copy-start | bytes 147460

commit v3 on v2

v3 whole, which is shorter than its diff:
```python
import jax
import jax.numpy as jnp
from jax import lax
from jax.experimental import pallas as pl
from jax.experimental.pallas import tpu as pltpu
from jax.sharding import PartitionSpec as P

F32 = jnp.float32
BF16 = jnp.bfloat16
MESH = pl.DeviceIdType.MESH
EPS = 1e-5
GRP, ROW = 8, 16
BR, KS, BLK, CZ, CH = 4, 6, 128, 128, 64
NB = BR * KS
QC = CH // ROW
PAD = 128
STEP = 2
VOFF = 64
PARTS = ((0, 6), (6, 10), (16, 8))
ROW_ORDER = (1, 3, 4, 12, 2, 8, 5, 15, 7, 13, 6, 14, 9, 11, 10)
GRP_ORDER = (2, 6, 4, 3, 7, 5, 1)


def row_peer(row, offset):
    z, y = row // 4, row % 4
    return ((z + offset // 4) % 4) * 4 + (y + offset % 4) % 4


def grp_peer(grp, offset):
    x, core = grp // 2, grp % 2
    return ((x + offset // 2) % 4) * 2 + (core + offset % 2) % 2


def layer_norm(values):
    center = jnp.mean(values, axis=-1, keepdims=True)
    shifted = values - center
    spread = jnp.mean(shifted * shifted, axis=-1, keepdims=True)
    inverse = lax.rsqrt(spread + EPS)
    return shifted * inverse, inverse


def dot_nt(a, b):
    return lax.dot_general(a, b, (((1,), (1,)), ((), ())), preferred_element_type=F32)


def dot_nn(a, b):
    return lax.dot_general(a, b, (((1,), (0,)), ((), ())), preferred_element_type=F32)


def dot_tn(a, b):
    return lax.dot_general(a, b, (((0,), (0,)), ((), ())), preferred_element_type=F32)


def i32(flag):
    return jnp.where(flag, 1, 0).astype(jnp.int32)


def named_ranks(cols, reader, owner):
    flags = [jnp.int32(0)] * BR
    for r in range(BR):
        for s in range(KS):
            c = cols[s, reader * BR + r]
            for l in range(BR):
                flags[l] = flags[l] | i32(c == owner * BR + l)
    ranks, count = [], jnp.int32(0)
    firsts = [jnp.int32(0), jnp.int32(0)]
    for l in range(BR):
        ranks.append(count)
        for a in range(2):
            firsts[a] = firsts[a] + l * flags[l] * i32(count == a)
        count = count + flags[l]
    return ranks, firsts


def pick(entries, index):
    out = jnp.int32(0)
    for n, entry in enumerate(entries):
        out = out + entry * i32(index == n)
    return out


def write_places(cols, grp, step, place, kvplace):
    inner = step // KS
    slot = step % KS
    j = cols[slot, grp * BR + inner]
    owner = j >> 2
    own = owner == grp
    ranks, _ = named_ranks(cols, grp, owner)
    offset = ((grp // 2 - owner // 2 + 4) % 4) * 2 + (grp % 2 - owner % 2 + 2) % 2
    rank_j = pick(ranks, j & 3)
    theirs = [cols[u, j] for u in range(KS)]
    for t in range(KS):
        c = cols[t, grp * BR + inner]
        found, far, count = jnp.int32(-1), jnp.int32(0), jnp.int32(0)
        for u in range(KS):
            hit = theirs[u] == c
            found = jnp.where(hit, u, found)
            far = jnp.where(hit, count, far)
            count = count + i32((theirs[u] >> 2) != owner)
        n = jnp.where((c >> 2) == owner, pick(ranks, c & 3), 2 + far)
        remote = NB + (offset - 1) * 8 + rank_j * 4 + n
        place[step * KS + t] = jnp.where(
            found >= 0, jnp.where(own, (j & 3) * KS + found, remote), NB + 56
        )
    kvplace[step] = jnp.where(own, j & 3, BR + (offset - 1) * 2 + rank_j)


def write_stages(cols, grp, to, stage, kvstage):
    reader = grp_peer(grp, to)
    _, firsts = named_ranks(cols, reader, grp)
    for a in range(2):
        near, far = [jnp.int32(0)] * 2, [jnp.int32(0)] * 2
        count = jnp.int32(0)
        for u in range(KS):
            c = cols[u, grp * BR + firsts[a]]
            away = i32((c >> 2) != grp)
            for n in range(2):
                near[n] = near[n] + u * i32(c == grp * BR + firsts[n])
                far[n] = far[n] + u * away * i32(count == n)
            count = count + away
        for n in range(2):
            stage[(to - 1) * 8 + a * 4 + n] = firsts[a] * KS + near[n]
            stage[(to - 1) * 8 + a * 4 + 2 + n] = firsts[a] * KS + far[n]
        kvstage[(to - 1) * 2 + a] = firsts[a]


def exchange_kernel(*refs):
    (
        cols, mask, chain, same, pair, tri_w, gate_w, bias_w, nodes, cotan, q_w, k_w, v_w, o_w,
        tri_out, grad_out, node_out, normed_out, gate_out, scale_out,
    ) = refs[:20]
    scr = list(refs[20:])
    take = lambda n: [scr.pop(0) for _ in range(n)]
    right = take(QC)
    left = take(QC)
    tri = take(QC)
    xs = take(QC)
    xr = take(QC)
    first_s = take(len(PARTS))
    rest_s = take(len(PARTS))
    left_s, bias_s = take(2)
    pair_v = take(len(PARTS))
    normed_v = take(len(PARTS))
    weights, ones, turned, shifted, inverse, gates, first_w, rest_w, place, kvplace, stage, kvstage = take(12)
    (bias, grads, kv_own, kv_s, kv_r, kv_all, queries, cots, mixed, mixed_r, wo_all,
     wq_pad, wkv_pad, wo_pad, scores, gprobs) = take(16)
    (right_ss, right_rs, left_ss, left_rs, tri_ss, tri_rs, x_ss, x_rs,
     kv_ss, kv_rs, grad_ss, grad_rs, mix_ss, mix_rs, wo_ss, wo_rs, bias_ss, bias_rs, own_s, pair_s, wx_ss, wx_rs, save_s) = take(23)

    grp = lax.axis_index("grp")
    row = lax.axis_index("row")
    mine = pl.ds(pl.multiple_of(row * 8, 8), 8)

    def to_row(src, dst, ss, rs, peer):
        return pltpu.make_async_remote_copy(
            src, dst, ss, rs, device_id=(grp, peer), device_id_type=MESH
        )

    def to_grp(src, dst, ss, rs, peer):
        return pltpu.make_async_remote_copy(
            src, dst, ss, rs, device_id=(peer, row), device_id_type=MESH
        )

    loads = [
        pltpu.make_async_copy(pair.at[pl.ds(first, count)], pair_v[h], pair_s.at[h])
        for h, (first, count) in enumerate(PARTS)
    ]
    for c in loads:
        c.start()

    barrier = pltpu.get_barrier_semaphore()
    for offset in ROW_ORDER:
        pl.semaphore_signal(barrier, inc=1, device_id=(grp, row_peer(row, offset)), device_id_type=MESH)
    for offset in GRP_ORDER:
        pl.semaphore_signal(barrier, inc=1, device_id=(grp_peer(grp, offset), row), device_id_type=MESH)
    wo_all[...] = jnp.zeros_like(wo_all)
    wo_pad[...] = jnp.zeros_like(wo_pad)
    weights[: 4 * CH, :] = (tri_w[...].astype(F32).T * 0.5).astype(BF16)
    weights[4 * CH :, :] = bias_w[...]
    ones[...] = jnp.full_like(ones, 1.0 / CZ)

    gates[...] = gate_w[...] * 0.5
    first_w[:ROW] = weights[2 * CH : 2 * CH + ROW]
    first_w[ROW:] = weights[3 * CH : 3 * CH + ROW]
    rest_w[: CH - ROW] = weights[2 * CH + ROW : 3 * CH]
    rest_w[CH - ROW :] = weights[3 * CH + ROW : 4 * CH]

    peers = [row_peer(row, offset) for offset in ROW_ORDER]

    def to_all(part, q, src, n_part):
        first, count = part
        here = pl.ds(first, count)
        return [
            to_row(src(p), right[q].at[here, mine, :], right_ss.at[n_part, n], right_rs.at[n_part, n], p)
            for n, p in enumerate(peers)
        ] + [pltpu.make_async_copy(src(row), right[q].at[here, mine, :], own_s.at[2, n_part])]

    right_c = [[to_all(part, 0, lambda p: first_s[h].at[p], h) for h, part in enumerate(PARTS)]] + [
        [
            to_all(part, q, lambda p: rest_s[h].at[(q - 1) * ROW + p], q * len(PARTS) + h)
            for h, part in enumerate(PARTS)
        ]
        for q in range(1, QC)
    ]
    left_c = [
        [
            to_row(left_s.at[q * ROW + p], left[q].at[:, mine, :], left_ss.at[q, n], left_rs.at[q, n], p)
            for n, p in enumerate(peers)
        ]
        + [pltpu.make_async_copy(left_s.at[q * ROW + row], left[q].at[:, mine, :], own_s.at[1, QC + q])]
        for q in range(QC)
    ]
    bias_c = [
        to_row(bias_s.at[p], bias.at[:, mine, :], bias_ss.at[n], bias_rs.at[n], p) for n, p in enumerate(peers)
    ] + [pltpu.make_async_copy(bias_s.at[row], bias.at[:, mine, :], own_s.at[0, 2 * QC])]
    chip = grp // 2
    fetches = chip < 3
    sixth = pl.ds(pl.multiple_of(lax.rem(grp, 6) * BLK, BLK), BLK)
    head_rows = pl.ds(VOFF, 48)
    wo_c = [
        to_row(o_w.at[:, sixth], wo_all.at[row, head_rows, sixth], wo_ss.at[n], wo_rs.at[n], p)
        for n, p in enumerate(peers)
    ]
    wo_own = pltpu.make_async_copy(o_w.at[:, sixth], wo_all.at[row, head_rows, sixth], own_s.at[0, 2 * QC + 1])

    def start(copies):
        for c in copies:
            c.start()

    for h, (first, count) in enumerate(PARTS):
        loads[h].wait()

        @pl.loop(0, count)
        def _(b):
            values = pair_v[h][b].reshape(8 * BLK, CZ)
            inverse[...] = dot_nn(values, ones[...])
            shifted[...] = values.astype(F32) - inverse[...]
            inverse[...] = dot_nn((shifted[...] * shifted[...]).astype(BF16), ones[...])
            normed_v[h][b] = (shifted[...] * lax.rsqrt(inverse[...] + EPS)).astype(BF16)
            for i in range(8):
                normed = normed_v[h][b, i * BLK : (i + 1) * BLK, :]
                projected = dot_nt(first_w[...], normed)
                turned[pl.ds(i, ROW, stride=8), :] = (jnp.tanh(projected[ROW:]) + 1.0) * projected[:ROW]
            first_s[h][:, b] = turned[: 8 * ROW].reshape(ROW, 8, BLK).astype(BF16)

        if h == 0:
            pl.semaphore_wait(barrier, 22)
        start(right_c[0][h])

    def project_rest(h):
        first, count = PARTS[h]

        @pl.loop(0, count)
        def _(b):
            for i in range(8):
                normed = normed_v[h][b, i * BLK : (i + 1) * BLK, :]
                projected = dot_nt(rest_w[...], normed)
                turned[pl.ds(i, CH - ROW, stride=8), :] = (
                    jnp.tanh(projected[CH - ROW :]) + 1.0
                ) * projected[: CH - ROW]
            rest_s[h][:, b] = turned[: 8 * (CH - ROW)].reshape(CH - ROW, 8, BLK).astype(BF16)

        for q in range(1, QC):
            start(right_c[q][h])

    project_rest(0)

    @pl.loop(1, GRP)
    def _(to):
        write_stages(cols, grp, to, stage, kvstage)

    saves = [
        pltpu.make_async_copy(normed_v[h], normed_out.at[pl.ds(first, count)], save_s.at[0, h])
        for h, (first, count) in enumerate(PARTS)
    ]
    start(saves)

    gpeers = [grp_peer(grp, offset) for offset in GRP_ORDER]
    x_c = []

    def exchange_channel(q):
        for part in right_c[q]:
            for c in part:
                c.wait()

        @pl.loop(0, 56)
        def _(n):
            xs[q][n] = right[q][stage[n]]

        x_c.append([
            to_grp(
                xs[q].at[pl.ds((o - 1) * 8, 8)], xr[q].at[pl.ds((o - 1) * 8, 8)],
                x_ss.at[q, n], x_rs.at[q, n], gpeers[n],
            )
            for n, o in enumerate(GRP_ORDER)
        ])
        start(x_c[q])

    exchange_channel(0)
    for h in range(1, len(PARTS)):
        project_rest(h)

    wq_pad[...] = jnp.zeros_like(wq_pad)
    wkv_pad[...] = jnp.zeros_like(wkv_pad)
    wq_pad[:48, :] = q_w[...]
    wkv_pad[:48, :] = k_w[...]
    wkv_pad[VOFF : VOFF + 48, :] = v_w[...]
    wo_pad[VOFF : VOFF + 48, :] = o_w[...]

    @pl.loop(0, BR)
    def _(r):
        part = pl.ds(pl.multiple_of(r * BLK, BLK), BLK)
        normed = layer_norm(nodes[part, :].astype(F32))[0].astype(BF16)
        queries[r] = dot_nt(normed, wq_pad[...]).astype(BF16)
        kv_own[r] = dot_nt(normed, wkv_pad[...]).astype(BF16)
        cots[r] = dot_nt(cotan[part, :], wo_pad[...]).astype(BF16)

    for n in range(14):
        kv_s[n] = kv_own[kvstage[n]]
    kv_c = [
        to_grp(kv_s.at[pl.ds((o - 1) * 2, 2)], kv_r.at[pl.ds((o - 1) * 2, 2)], kv_ss.at[n], kv_rs.at[n], gpeers[n])
        for n, o in enumerate(GRP_ORDER)
    ]
    start(kv_c)

    for h, (first, count) in enumerate(PARTS):

        @pl.loop(0, count)
        def _(b):
            for i in range(8):
                normed = normed_v[h][b, i * BLK : (i + 1) * BLK, :]
                projected = dot_nt(weights[: 2 * CH, :], normed)
                turned[pl.ds(i, CH, stride=8), :] = (jnp.tanh(projected[CH:]) + 1.0) * projected[:CH]
                turned[pl.ds(8 * CH + i, ROW, stride=8), :] = dot_nt(weights[4 * CH :, :], normed)
            left_s[:, first + b] = turned[: 8 * CH].reshape(CH, 8, BLK).astype(BF16)
            bias_s[:, first + b] = turned[8 * CH :].reshape(ROW, 8, BLK).astype(BF16)

    start(bias_c)
    for q in range(QC):
        start(left_c[q])

    @pl.when(fetches)
    def _():
        start(wo_c + [wo_own])

    exchange_channel(1)

    for h, (first, count) in enumerate(PARTS):

        @pl.loop(0, count)
        def _(b):
            values = pair_v[h][b].reshape(8 * BLK, CZ)
            shifted[...] = values.astype(F32) - dot_nn(values, ones[...])
            squares = (shifted[...] * shifted[...]).astype(BF16)
            for i in range(8):
                spread = dot_nt(ones[:8], squares[i * BLK : (i + 1) * BLK])
                scale_out[first + b, i : i + 1, :] = lax.rsqrt(spread[:1] + EPS)
            inverse[...] = jnp.tanh(dot_nn(normed_v[h][b], gates[...])) + 1.0
            pair_v[h][b] = inverse[...].astype(BF16).reshape(8, BLK, CZ)

        saves.append(pltpu.make_async_copy(pair_v[h], gate_out.at[pl.ds(first, count)], save_s.at[1, h]))
        saves[-1].start()

    exchange_channel(2)
    exchange_channel(3)

    @pl.loop(0, NB)
    def _(b):
        write_places(cols, grp, b, place, kvplace)

    for c in kv_c:
        c.wait()
    for c in bias_c:
        c.wait()
    kv_all[:BR] = kv_own[...]
    kv_all[BR:] = kv_r[...]
    chain_bias = same[row]

    @pl.loop(0, BR)
    def _(r):
        here = chain[grp * BR + r]
        query = queries[r]
        cot = cots[r]
        top = jnp.full((BLK, 1), -jnp.inf, F32)
        for s in range(KS):
            kv = kv_all[kvplace[r * KS + s]]
            j = cols[s, grp * BR + r]
            extra = jnp.where(chain[j] == here, chain_bias, 0.0)
            part = dot_nt(query, kv) * (48 ** -0.5) + (bias[r * KS + s].astype(F32) + extra)
            part = jnp.where(mask[s, grp * BR + r] > 0, part, -jnp.inf)
            scores[s] = part
            gprobs[s] = dot_nt(cot, kv)
            top = jnp.maximum(top, jnp.max(part, axis=1, keepdims=True))
        total = jnp.zeros((BLK, 1), F32)
        for s in range(KS):
            part = jnp.exp(scores[s] - top)
            scores[s] = part
            total = total + jnp.sum(part, axis=1, keepdims=True)
        inverse = 1.0 / total
        dots = jnp.zeros((BLK, 1), F32)
        mix = jnp.zeros((BLK, PAD), F32)
        for s in range(KS):
            probs = scores[s] * inverse
            scores[s] = probs
            dots = dots + jnp.sum(probs * gprobs[s], axis=1, keepdims=True)
            mix = mix + dot_nn(probs.astype(BF16), kv_all[kvplace[r * KS + s]])
        for s in range(KS):
            grads[r * KS + s] = (scores[s] * (gprobs[s] - dots)).astype(BF16)
        mixed[pl.ds(pl.multiple_of(r * BLK, BLK), BLK), :] = mix.astype(BF16)

    slot = lambda p: pl.ds(pl.multiple_of(p * 8, 8), 8)
    rows32 = lambda p: pl.ds(pl.multiple_of(p * 32, 32), 32)
    mix_c = [
        to_row(mixed.at[rows32(p)], mixed_r.at[row], mix_ss.at[n], mix_rs.at[n], p) for n, p in enumerate(peers)
    ]
    mix_own = pltpu.make_async_copy(mixed.at[rows32(row)], mixed_r.at[row], own_s.at[0, 2 * QC + 2])
    grad_c = [
        to_row(grads.at[:, slot(p), :], grad_out.at[:, row], grad_ss.at[n], grad_rs.at[n], p)
        for n, p in enumerate(peers)
    ]
    grad_own = pltpu.make_async_copy(grads.at[:, mine, :], grad_out.at[:, row], own_s.at[0, 2 * QC + 3])
    for c in mix_c + [mix_own] + grad_c + [grad_own]:
        c.start()

    tri_c = []
    wx_c = [
        to_grp(wo_all.at[:, head_rows, sixth], wo_all.at[:, head_rows, sixth], wx_ss.at[n], wx_rs.at[n], gpeers[n])
        for n in range(7)
    ]
    for q in range(QC):
        if q == QC - 1:

            @pl.when(fetches)
            def _():
                for c in wo_c + [wo_own]:
                    c.wait()
                for c in wx_c:
                    c.start()

        for c in left_c[q]:
            c.wait()
        for c in x_c[q]:
            c.wait()

        cuts = ((0, NB),) if q < QC - 1 else ((0, NB // 2), (NB // 2, NB // 2))
        for h, (first, count) in enumerate(cuts):

            @pl.loop(first, first + count)
            def _(b):
                r = b // KS
                lhs, rhs = [], []
                for t in range(KS):
                    code = place[b * KS + t]
                    near = right[q][jnp.minimum(code, NB - 1)]
                    far = xr[q][jnp.clip(code - NB, 0, 55)]
                    block = jnp.where(code < NB, near, far)
                    rhs.append(jnp.where(code < NB + 56, block, jnp.zeros_like(block)))
                    lhs.append(left[q][r * KS + t])
                tri[q][b] = dot_nt(jnp.concatenate(lhs, axis=1), jnp.concatenate(rhs, axis=1)).astype(BF16)

            here = pl.ds(first, count)
            tri_c.append([
                to_row(tri[q].at[here, slot(p), :], tri_out.at[here, q, row], tri_ss.at[q + h, n], tri_rs.at[q + h, n], p)
                for n, p in enumerate(peers)
            ] + [pltpu.make_async_copy(tri[q].at[here, mine, :], tri_out.at[here, q, row], own_s.at[1, 8 + q + h])])
            start(tri_c[-1])

    for c in mix_c + [mix_own]:
        c.wait()

    @pl.when(fetches)
    def _():
        for c in wx_c:
            c.wait_send()

    for n, o in enumerate(GRP_ORDER):

        @pl.when((chip - o // 2 + 4) % 4 < 3)
        def _():
            wx_c[n].wait_recv()

    acc = nodes[rows32(row), :].astype(F32)
    for p in range(ROW):
        acc = acc + dot_nn(mixed_r[p], wo_all[p])
    node_out[...] = acc.astype(BF16)

    for c in saves + grad_c + [grad_own]:
        c.wait()
    for part in tri_c:
        for c in part:
            c.wait()


def exchange(scalars, tensors, nodes):
    smem = pl.BlockSpec(memory_space=pltpu.SMEM)
    vmem = pl.BlockSpec(memory_space=pltpu.VMEM)
    anyspace = pl.BlockSpec(memory_space=pl.ANY)
    dma = pltpu.SemaphoreType.DMA
    blocks = lambda n: pltpu.VMEM((n, BLK, BLK), BF16)
    blocks_2d = pltpu.VMEM((BLK, BLK), BF16)
    n = ROW - 1
    scratch = (
        [blocks(NB)] * QC + [blocks(NB)] * QC + [blocks(NB)] * QC + [blocks(56)] * QC + [blocks(56)] * QC
        + [pltpu.VMEM((ROW, k, 8, BLK), BF16) for _, k in PARTS]
        + [pltpu.VMEM((CH - ROW, k, 8, BLK), BF16) for _, k in PARTS]
        + [pltpu.VMEM((CH, NB, 8, BLK), BF16), pltpu.VMEM((ROW, NB, 8, BLK), BF16)]
        + [pltpu.VMEM((k, 8, BLK, CZ), BF16) for _, k in PARTS]
        + [pltpu.VMEM((k, 8 * BLK, CZ), BF16) for _, k in PARTS]
        + [
            pltpu.VMEM((4 * CH + ROW, CZ), BF16), blocks_2d, pltpu.VMEM(((CH + ROW) * 8, BLK), F32),
            pltpu.VMEM((8 * BLK, CZ), F32), pltpu.VMEM((8 * BLK, CZ), F32), blocks_2d,
            pltpu.VMEM((2 * ROW, CZ), BF16), pltpu.VMEM((2 * (CH - ROW), CZ), BF16),
            pltpu.SMEM((NB * KS,), jnp.int32), pltpu.SMEM((NB,), jnp.int32),
            pltpu.SMEM((56,), jnp.int32), pltpu.SMEM((14,), jnp.int32),
        ]
        + [
            blocks(NB), blocks(NB), blocks(BR), blocks(14), blocks(14), blocks(BR + 14), blocks(BR), blocks(BR),
            pltpu.VMEM((BR * BLK, PAD), BF16), pltpu.VMEM((ROW, 32, PAD), BF16),
            pltpu.VMEM((ROW, PAD, 768), BF16), pltpu.VMEM((PAD, 768), BF16), pltpu.VMEM((PAD, 768), BF16),
            pltpu.VMEM((PAD, 768), BF16), pltpu.VMEM((KS, BLK, BLK), F32), pltpu.VMEM((KS, BLK, BLK), F32),
        ]
        + [dma((len(PARTS) * QC, n))] * 2 + [dma((QC, n))] * 2 + [dma((QC + 1, n))] * 2 + [dma((QC, 7))] * 2 + [dma((7,))] * 2 + [dma((n,))] * 8
        + [dma((len(PARTS), 2 * QC + 1 + QC)), dma((len(PARTS),)), dma((7,)), dma((7,)), dma((2, len(PARTS)))]
    )
    return pl.pallas_call(
        exchange_kernel,
        in_specs=[smem] * 4 + [anyspace] + [vmem] * 9,
        out_specs=[anyspace, anyspace, vmem, anyspace, anyspace, vmem],
        out_shape=[
            jax.ShapeDtypeStruct((NB, QC, ROW, 8, BLK), BF16),
            jax.ShapeDtypeStruct((NB, ROW, 8, BLK), BF16),
            jax.ShapeDtypeStruct((32, 768), BF16),
            jax.ShapeDtypeStruct((NB, 8 * BLK, CZ), BF16),
            jax.ShapeDtypeStruct((NB, 8, BLK, CZ), BF16),
            jax.ShapeDtypeStruct((NB, 8, BLK), F32),
        ],
        scratch_shapes=scratch,
        compiler_params=pltpu.CompilerParams(
            collective_id=0, has_side_effects=True, vmem_limit_bytes=63 << 20
        ),
        name="exchange",
    )(*scalars, *tensors, *nodes)


def finish_kernel(
    pair, tri, grads, normed, gate, scale, out_w, bias_w, pair_out, pair_grad,
    weights, ones, turned, hidden, both, along,
):
    @pl.when(pl.program_id(0) == 0)
    def _():
        bias = bias_w[...].astype(F32)
        weights[...] = jnp.zeros_like(weights)
        weights[:CH, :CZ] = out_w[...] * 0.5
        weights[CH : CH + ROW, CZ:] = (bias - jnp.mean(bias, axis=1, keepdims=True)).astype(BF16)
        ones[...] = jnp.full_like(ones, 1.0 / CZ)
        turned[...] = jnp.zeros_like(turned)

    def norm(k):
        sums = tri[k].astype(F32)
        centred = sums - jnp.mean(sums, axis=0, keepdims=True)
        spread = jnp.mean(centred * centred, axis=0, keepdims=True)
        turned[k, : 8 * CH] = (centred * lax.rsqrt(spread + EPS)).reshape(8 * CH, BLK)
        turned[k, 8 * CH : 8 * (CH + ROW)] = (grads[k].astype(F32) * scale[k]).reshape(8 * ROW, BLK)

    def turn(k):
        for i in range(8):
            hidden[k, i * BLK : (i + 1) * BLK, :] = turned[k, pl.ds(i, PAD, stride=8), :].astype(BF16).T

    def product(k):
        both[k] = dot_nn(hidden[k], weights[...])

    def project(k):
        along[k] = dot_nn(both[k, :, CZ:].astype(BF16) * normed[k], ones[...])

    def store(k):
        for i in range(8):
            rows = slice(i * BLK, (i + 1) * BLK)
            pair_out[k, i] = (
                pair[k, i].astype(F32) + gate[k, i].astype(F32) * both[k, rows, :CZ]
            ).astype(BF16)
            pair_grad[k, i] = (
                both[k, rows, CZ:] - normed[k, rows, :].astype(F32) * along[k, rows, :]
            ).astype(BF16)

    norm(0)
    for k in range(STEP):
        turn(k)
        if k + 1 < STEP:
            norm(k + 1)
        product(k)
        if k > 0:
            store(k - 1)
        project(k)
    store(STEP - 1)


def finish(pair, tri, grads, normed, gate, scale, out_w, bias_w):
    by_block = lambda a: pl.BlockSpec((STEP,) + a.shape[1:], lambda b: (b,) + (0,) * (a.ndim - 1))
    whole = lambda a: pl.BlockSpec(a.shape, lambda b: (0,) * a.ndim)
    return pl.pallas_call(
        finish_kernel,
        grid=(NB // STEP,),
        in_specs=[by_block(a) for a in (pair, tri, grads, normed, gate, scale)] + [whole(out_w), whole(bias_w)],
        out_specs=[by_block(pair), by_block(pair)],
        out_shape=[jax.ShapeDtypeStruct(pair.shape, BF16)] * 2,
        scratch_shapes=[
            pltpu.VMEM((PAD, 2 * CZ), BF16),
            pltpu.VMEM((CZ, CZ), BF16),
            pltpu.VMEM((STEP, PAD * 8, BLK), F32),
            pltpu.VMEM((STEP, 8 * BLK, PAD), BF16),
            pltpu.VMEM((STEP, 8 * BLK, 2 * CZ), F32),
            pltpu.VMEM((STEP, 8 * BLK, CZ), F32),
        ],
        compiler_params=pltpu.CompilerParams(vmem_limit_bytes=62 << 20),
        name="finish",
    )(pair, tri, grads, normed, gate, scale, out_w, bias_w)


def per_device(
    pair_feats,
    block_cols,
    attn_mask,
    chain_of_row,
    same_chain,
    node_feats,
    node_cotangent,
    tri_weight,
    gate_weight,
    tri_out_weight,
    bias_weight,
    query_weight,
    key_weight,
    value_weight,
    out_weight,
):
    pair = pair_feats.reshape(NB, 8, BLK, CZ)
    bias_t = bias_weight.T
    tri, grads, node_out, normed, gate, scale = exchange(
        (block_cols.T, attn_mask.T, chain_of_row, same_chain),
        (pair, tri_weight, gate_weight, bias_t),
        (node_feats, node_cotangent, query_weight.T, key_weight.T, value_weight.T, out_weight),
    )
    pair_out, pair_grad = finish(
        pair, tri.reshape(NB, CH, 8, BLK), grads, normed, gate, scale, tri_out_weight, bias_t
    )
    return pair_out.reshape(pair_feats.shape), node_out, pair_grad.reshape(pair_feats.shape)


def solution(mesh):
    pair_spec = P("grp", None, "row", None, None)
    node_spec = P("grp", None)
    in_specs = (
        (pair_spec,) + (P(),) * 4 + (node_spec,) * 2 + (P(),) * 4 + (P(None, "row"),) * 3 + (P("row", None),)
    )
    out_specs = (pair_spec, P(("grp", "row"), None), pair_spec)
    return jax.shard_map(per_device, mesh=mesh, in_specs=in_specs, out_specs=out_specs, check_vma=False)
```

time: 189 us -> 175 us (0.926)
  Pallas kernels: 187 us -> 173 us
    pallas_call x1, Pallas kernels: 162 us -> 154 us  [exchange(): pl.pallas_call(exchange_kernel, in_specs=[smem] * 4 + [anyspace] + [vmem]...]
    pallas_call x1, Pallas kernels: 25.2 us -> 19.9 us  [finish(): pl.pallas_call(finish_kernel, grid=(NB // STEP,), in_specs=[by_block(a) f...]
where the time goes in v3:
time: 175 us
  Pallas kernels  173 us (99%)
    pallas_call x1, Pallas kernels, exchange(): pl.pallas_call(exchange_kernel, in_specs=[smem] * 4 + [anyspace] + [vmem]...  154 us
    pallas_call x1, Pallas kernels, finish(): pl.pallas_call(finish_kernel, grid=(NB // STEP,), in_specs=[by_block(a) f...  19.9 us

profile of v3, /device:TPU:1, one launch (start us, length us, event | category | flops | bytes accessed | tf_op | source)
XLA Modules:
  0.0 174.7 jit_solution(8441122235224703080)
XLA Ops:
  0.6 153.5 %exchange.1 = (bf16[24,4,16,8,128]{4,3,2,1,0:T(8,128)(2,1)}, bf16[24,16,8,128]{3,2,1,0:T(8,128)(2,1)}, bf16[32,768]{1,0:T(8,128)(2,1)}, bf16[24,1024,128]{2,1,0:...) custom-call(s32[6,32]{1,0:T(8,128)} %bitcast.18, s32[6,32]{1,0:T(8,128)} %bitcast.19, s32[32]{0:T(128)} %refs_2_.1, ...), custom_call_target="tpu_custom_call" | custom-call | tf_op jit(solution)/shard_map/exchange/pallas_call | solution.py:525
  154.1 0.0 copy-start
  154.2 19.9 %finish.1 = (bf16[24,8,128,128]{3,2,1,0:T(8,128)(2,1)}, bf16[24,8,128,128]{3,2,1,0:T(8,128)(2,1)}) custom-call(bf16[24,8,128,128]{3,2,1,0:T(8,128)(2,1)} %bitcast.11, bf16[24,64,8,128]{3,2,1,0:T(8,128)(2,1)} %bitcast.12, bf16[24,16,8,128]{3,2,1,0:T(8,128)(2,1)} %get-tuple-element.12.grads, bf16[24,1024,128]{2,1,0:T(8,128)(2,1)} %get-tuple-element.13.normed, ...), custom_call_target="tpu_custom_call" | custom-call | tf_op jit(solution)/shard_map/finish/pallas_call | solution.py:600
  174.1 0.0 copy-done
  174.1 0.6 copy.19
Async XLA Ops:
  154.1 19.9 %copy-start = (bf16[32,768]{1,0:T(8,128)(2,1)S(1)}, bf16[32,768]{1,0:T(8,128)(2,1)}, u32[]{:S(2)}) copy-start(bf16[32,768]{1,0:T(8,128)(2,1)} %get-tuple-element.23) | copy-start | bytes 147460

commit v4 on v3

--- a/solution.py
+++ b/solution.py
@@ -173,8 +173,6 @@
         pl.semaphore_signal(barrier, inc=1, device_id=(grp, row_peer(row, offset)), device_id_type=MESH)
     for offset in GRP_ORDER:
         pl.semaphore_signal(barrier, inc=1, device_id=(grp_peer(grp, offset), row), device_id_type=MESH)
-    wo_all[...] = jnp.zeros_like(wo_all)
-    wo_pad[...] = jnp.zeros_like(wo_pad)
     weights[: 4 * CH, :] = (tri_w[...].astype(F32).T * 0.5).astype(BF16)
     weights[4 * CH :, :] = bias_w[...]
     ones[...] = jnp.full_like(ones, 1.0 / CZ)
@@ -216,16 +214,63 @@
     chip = grp // 2
     fetches = chip < 3
     sixth = pl.ds(pl.multiple_of(lax.rem(grp, 6) * BLK, BLK), BLK)
-    head_rows = pl.ds(VOFF, 48)
     wo_c = [
-        to_row(o_w.at[:, sixth], wo_all.at[row, head_rows, sixth], wo_ss.at[n], wo_rs.at[n], p)
+        to_row(o_w.at[:, sixth], wo_all.at[row, :, sixth], wo_ss.at[n], wo_rs.at[n], p)
         for n, p in enumerate(peers)
     ]
-    wo_own = pltpu.make_async_copy(o_w.at[:, sixth], wo_all.at[row, head_rows, sixth], own_s.at[0, 2 * QC + 1])
+    wo_own = pltpu.make_async_copy(o_w.at[:, sixth], wo_all.at[row, :, sixth], own_s.at[0, 2 * QC + 1])
 
     def start(copies):
         for c in copies:
             c.start()
+
+    def project_rest(h):
+        first, count = PARTS[h]
+
+        @pl.loop(0, count)
+        def _(b):
+            for i in range(8):
+                normed = normed_v[h][b, i * BLK : (i + 1) * BLK, :]
+                projected = dot_nt(rest_w[...], normed)
+                turned[pl.ds(i, CH - ROW, stride=8), :] = (
+                    jnp.tanh(projected[CH - ROW :]) + 1.0
+                ) * projected[: CH - ROW]
+            rest_s[h][:, b] = turned[: 8 * (CH - ROW)].reshape(CH - ROW, 8, BLK).astype(BF16)
+
+        for q in range(1, QC):
+            start(right_c[q][h])
+
+    gpeers = [grp_peer(grp, offset) for offset in GRP_ORDER]
+    kv_c = []
+
+    def node_part():
+        @pl.loop(1, GRP)
+        def _(to):
+            write_stages(cols, grp, to, stage, kvstage)
+
+        wo_pad[...] = jnp.zeros_like(wo_pad)
+        wq_pad[...] = jnp.zeros_like(wq_pad)
+        wkv_pad[...] = jnp.zeros_like(wkv_pad)
+        wq_pad[:48, :] = q_w[...]
+        wkv_pad[:48, :] = k_w[...]
+        wkv_pad[VOFF : VOFF + 48, :] = v_w[...]
+        wo_pad[VOFF : VOFF + 48, :] = o_w[...]
+
+        @pl.loop(0, BR)
+        def _(r):
+            part = pl.ds(pl.multiple_of(r * BLK, BLK), BLK)
+            normed = layer_norm(nodes[part, :].astype(F32))[0].astype(BF16)
+            queries[r] = dot_nt(normed, wq_pad[...]).astype(BF16)
+            kv_own[r] = dot_nt(normed, wkv_pad[...]).astype(BF16)
+            cots[r] = dot_nt(cotan[part, :], wo_pad[...]).astype(BF16)
+
+        for n in range(14):
+            kv_s[n] = kv_own[kvstage[n]]
+        kv_c[:] = [
+            to_grp(kv_s.at[pl.ds((o - 1) * 2, 2)], kv_r.at[pl.ds((o - 1) * 2, 2)], kv_ss.at[n], kv_rs.at[n], gpeers[n])
+            for n, o in enumerate(GRP_ORDER)
+        ]
+        start(kv_c)
 
     for h, (first, count) in enumerate(PARTS):
         loads[h].wait()
@@ -246,28 +291,10 @@
         if h == 0:
             pl.semaphore_wait(barrier, 22)
         start(right_c[0][h])
-
-    def project_rest(h):
-        first, count = PARTS[h]
-
-        @pl.loop(0, count)
-        def _(b):
-            for i in range(8):
-                normed = normed_v[h][b, i * BLK : (i + 1) * BLK, :]
-                projected = dot_nt(rest_w[...], normed)
-                turned[pl.ds(i, CH - ROW, stride=8), :] = (
-                    jnp.tanh(projected[CH - ROW :]) + 1.0
-                ) * projected[: CH - ROW]
-            rest_s[h][:, b] = turned[: 8 * (CH - ROW)].reshape(CH - ROW, 8, BLK).astype(BF16)
-
-        for q in range(1, QC):
-            start(right_c[q][h])
-
-    project_rest(0)
-
-    @pl.loop(1, GRP)
-    def _(to):
-        write_stages(cols, grp, to, stage, kvstage)
+        if h == 0:
+            project_rest(0)
+            node_part()
+
 
     saves = [
         pltpu.make_async_copy(normed_v[h], normed_out.at[pl.ds(first, count)], save_s.at[0, h])
@@ -275,7 +302,6 @@
     ]
     start(saves)
 
-    gpeers = [grp_peer(grp, offset) for offset in GRP_ORDER]
     x_c = []
 
     def exchange_channel(q):
@@ -299,29 +325,6 @@
     exchange_channel(0)
     for h in range(1, len(PARTS)):
         project_rest(h)
-
-    wq_pad[...] = jnp.zeros_like(wq_pad)
-    wkv_pad[...] = jnp.zeros_like(wkv_pad)
-    wq_pad[:48, :] = q_w[...]
-    wkv_pad[:48, :] = k_w[...]
-    wkv_pad[VOFF : VOFF + 48, :] = v_w[...]
-    wo_pad[VOFF : VOFF + 48, :] = o_w[...]
-
-    @pl.loop(0, BR)
-    def _(r):
-        part = pl.ds(pl.multiple_of(r * BLK, BLK), BLK)
-        normed = layer_norm(nodes[part, :].astype(F32))[0].astype(BF16)
-        queries[r] = dot_nt(normed, wq_pad[...]).astype(BF16)
-        kv_own[r] = dot_nt(normed, wkv_pad[...]).astype(BF16)
-        cots[r] = dot_nt(cotan[part, :], wo_pad[...]).astype(BF16)
-
-    for n in range(14):
-        kv_s[n] = kv_own[kvstage[n]]
-    kv_c = [
-        to_grp(kv_s.at[pl.ds((o - 1) * 2, 2)], kv_r.at[pl.ds((o - 1) * 2, 2)], kv_ss.at[n], kv_rs.at[n], gpeers[n])
-        for n, o in enumerate(GRP_ORDER)
-    ]
-    start(kv_c)
 
     for h, (first, count) in enumerate(PARTS):
 
@@ -424,7 +427,7 @@
 
     tri_c = []
     wx_c = [
-        to_grp(wo_all.at[:, head_rows, sixth], wo_all.at[:, head_rows, sixth], wx_ss.at[n], wx_rs.at[n], gpeers[n])
+        to_grp(wo_all.at[:, :, sixth], wo_all.at[:, :, sixth], wx_ss.at[n], wx_rs.at[n], gpeers[n])
         for n in range(7)
     ]
     for q in range(QC):
@@ -442,7 +445,7 @@
         for c in x_c[q]:
             c.wait()
 
-        cuts = ((0, NB),) if q < QC - 1 else ((0, NB // 2), (NB // 2, NB // 2))
+        cuts = ((0, NB),) if q < QC - 1 else tuple((r * KS, KS) for r in range(BR))
         for h, (first, count) in enumerate(cuts):
 
             @pl.loop(first, first + count)
@@ -481,7 +484,7 @@
 
     acc = nodes[rows32(row), :].astype(F32)
     for p in range(ROW):
-        acc = acc + dot_nn(mixed_r[p], wo_all[p])
+        acc = acc + dot_nn(mixed_r[p, :, VOFF : VOFF + 48], wo_all[p])
     node_out[...] = acc.astype(BF16)
 
     for c in saves + grad_c + [grad_own]:
@@ -516,11 +519,11 @@
         + [
             blocks(NB), blocks(NB), blocks(BR), blocks(14), blocks(14), blocks(BR + 14), blocks(BR), blocks(BR),
             pltpu.VMEM((BR * BLK, PAD), BF16), pltpu.VMEM((ROW, 32, PAD), BF16),
-            pltpu.VMEM((ROW, PAD, 768), BF16), pltpu.VMEM((PAD, 768), BF16), pltpu.VMEM((PAD, 768), BF16),
+            pltpu.VMEM((ROW, 48, 768), BF16), pltpu.VMEM((PAD, 768), BF16), pltpu.VMEM((PAD, 768), BF16),
             pltpu.VMEM((PAD, 768), BF16), pltpu.VMEM((KS, BLK, BLK), F32), pltpu.VMEM((KS, BLK, BLK), F32),
         ]
-        + [dma((len(PARTS) * QC, n))] * 2 + [dma((QC, n))] * 2 + [dma((QC + 1, n))] * 2 + [dma((QC, 7))] * 2 + [dma((7,))] * 2 + [dma((n,))] * 8
-        + [dma((len(PARTS), 2 * QC + 1 + QC)), dma((len(PARTS),)), dma((7,)), dma((7,)), dma((2, len(PARTS)))]
+        + [dma((len(PARTS) * QC, n))] * 2 + [dma((QC, n))] * 2 + [dma((QC - 1 + BR, n))] * 2 + [dma((QC, 7))] * 2 + [dma((7,))] * 2 + [dma((n,))] * 8
+        + [dma((len(PARTS), 2 * QC + BR + QC)), dma((len(PARTS),)), dma((7,)), dma((7,)), dma((2, len(PARTS)))]
     )
     return pl.pallas_call(
         exchange_kernel,
@@ -575,12 +578,8 @@
     def store(k):
         for i in range(8):
             rows = slice(i * BLK, (i + 1) * BLK)
-            pair_out[k, i] = (
-                pair[k, i].astype(F32) + gate[k, i].astype(F32) * both[k, rows, :CZ]
-            ).astype(BF16)
-            pair_grad[k, i] = (
-                both[k, rows, CZ:] - normed[k, rows, :].astype(F32) * along[k, rows, :]
-            ).astype(BF16)
+            pair_out[k, i] = pair[k, i] + gate[k, i] * both[k, rows, :CZ].astype(BF16)
+            pair_grad[k, i] = both[k, rows, CZ:].astype(BF16) - normed[k, rows, :] * along[k, rows, :].astype(BF16)
 
     norm(0)
     for k in range(STEP):

time: 175 us -> 177 us (1.011)
  Pallas kernels: 173 us -> 175 us
where the time goes in v4:
time: 177 us; the launch traced here: 176 us
  Pallas kernels  175 us (99%)
    pallas_call x1, Pallas kernels, exchange(): pl.pallas_call(exchange_kernel, in_specs=[smem] * 4 + [anyspace] + [vmem]...  155 us
    pallas_call x1, Pallas kernels, finish(): pl.pallas_call(finish_kernel, grid=(NB // STEP,), in_specs=[by_block(a) f...  19.9 us

profile of v4, /device:TPU:1, one launch (start us, length us, event | category | flops | bytes accessed | tf_op | source)
XLA Modules:
  0.0 175.8 jit_solution(13064783134485402630)
XLA Ops:
  0.6 154.6 %exchange.1 = (bf16[24,4,16,8,128]{4,3,2,1,0:T(8,128)(2,1)}, bf16[24,16,8,128]{3,2,1,0:T(8,128)(2,1)}, bf16[32,768]{1,0:T(8,128)(2,1)}, bf16[24,1024,128]{2,1,0:...) custom-call(s32[6,32]{1,0:T(8,128)} %bitcast.18, s32[6,32]{1,0:T(8,128)} %bitcast.19, s32[32]{0:T(128)} %refs_2_.1, ...), custom_call_target="tpu_custom_call" | custom-call | tf_op jit(solution)/shard_map/exchange/pallas_call | solution.py:528
  155.3 0.0 copy-start
  155.3 19.9 %finish.1 = (bf16[24,8,128,128]{3,2,1,0:T(8,128)(2,1)}, bf16[24,8,128,128]{3,2,1,0:T(8,128)(2,1)}) custom-call(bf16[24,8,128,128]{3,2,1,0:T(8,128)(2,1)} %bitcast.11, bf16[24,64,8,128]{3,2,1,0:T(8,128)(2,1)} %bitcast.12, bf16[24,16,8,128]{3,2,1,0:T(8,128)(2,1)} %get-tuple-element.12.grads, bf16[24,1024,128]{2,1,0:T(8,128)(2,1)} %get-tuple-element.13.normed, ...), custom_call_target="tpu_custom_call" | custom-call | tf_op jit(solution)/shard_map/finish/pallas_call | solution.py:599
  175.2 0.0 copy-done
  175.2 0.6 copy.19
Async XLA Ops:
  155.3 19.9 %copy-start = (bf16[32,768]{1,0:T(8,128)(2,1)S(1)}, bf16[32,768]{1,0:T(8,128)(2,1)}, u32[]{:S(2)}) copy-start(bf16[32,768]{1,0:T(8,128)(2,1)} %get-tuple-element.23) | copy-start | bytes 147460

commit v5 on v3

--- a/solution.py
+++ b/solution.py
@@ -173,7 +173,6 @@
         pl.semaphore_signal(barrier, inc=1, device_id=(grp, row_peer(row, offset)), device_id_type=MESH)
     for offset in GRP_ORDER:
         pl.semaphore_signal(barrier, inc=1, device_id=(grp_peer(grp, offset), row), device_id_type=MESH)
-    wo_all[...] = jnp.zeros_like(wo_all)
     wo_pad[...] = jnp.zeros_like(wo_pad)
     weights[: 4 * CH, :] = (tri_w[...].astype(F32).T * 0.5).astype(BF16)
     weights[4 * CH :, :] = bias_w[...]
@@ -216,12 +215,11 @@
     chip = grp // 2
     fetches = chip < 3
     sixth = pl.ds(pl.multiple_of(lax.rem(grp, 6) * BLK, BLK), BLK)
-    head_rows = pl.ds(VOFF, 48)
     wo_c = [
-        to_row(o_w.at[:, sixth], wo_all.at[row, head_rows, sixth], wo_ss.at[n], wo_rs.at[n], p)
+        to_row(o_w.at[:, sixth], wo_all.at[row, :, sixth], wo_ss.at[n], wo_rs.at[n], p)
         for n, p in enumerate(peers)
     ]
-    wo_own = pltpu.make_async_copy(o_w.at[:, sixth], wo_all.at[row, head_rows, sixth], own_s.at[0, 2 * QC + 1])
+    wo_own = pltpu.make_async_copy(o_w.at[:, sixth], wo_all.at[row, :, sixth], own_s.at[0, 2 * QC + 1])
 
     def start(copies):
         for c in copies:
@@ -424,7 +422,7 @@
 
     tri_c = []
     wx_c = [
-        to_grp(wo_all.at[:, head_rows, sixth], wo_all.at[:, head_rows, sixth], wx_ss.at[n], wx_rs.at[n], gpeers[n])
+        to_grp(wo_all.at[:, :, sixth], wo_all.at[:, :, sixth], wx_ss.at[n], wx_rs.at[n], gpeers[n])
         for n in range(7)
     ]
     for q in range(QC):
@@ -481,7 +479,7 @@
 
     acc = nodes[rows32(row), :].astype(F32)
     for p in range(ROW):
-        acc = acc + dot_nn(mixed_r[p], wo_all[p])
+        acc = acc + dot_nn(mixed_r[p, :, VOFF : VOFF + 48], wo_all[p])
     node_out[...] = acc.astype(BF16)
 
     for c in saves + grad_c + [grad_own]:
@@ -516,7 +514,7 @@
         + [
             blocks(NB), blocks(NB), blocks(BR), blocks(14), blocks(14), blocks(BR + 14), blocks(BR), blocks(BR),
             pltpu.VMEM((BR * BLK, PAD), BF16), pltpu.VMEM((ROW, 32, PAD), BF16),
-            pltpu.VMEM((ROW, PAD, 768), BF16), pltpu.VMEM((PAD, 768), BF16), pltpu.VMEM((PAD, 768), BF16),
+            pltpu.VMEM((ROW, 48, 768), BF16), pltpu.VMEM((PAD, 768), BF16), pltpu.VMEM((PAD, 768), BF16),
             pltpu.VMEM((PAD, 768), BF16), pltpu.VMEM((KS, BLK, BLK), F32), pltpu.VMEM((KS, BLK, BLK), F32),
         ]
         + [dma((len(PARTS) * QC, n))] * 2 + [dma((QC, n))] * 2 + [dma((QC + 1, n))] * 2 + [dma((QC, 7))] * 2 + [dma((7,))] * 2 + [dma((n,))] * 8
@@ -536,7 +534,7 @@
         ],
         scratch_shapes=scratch,
         compiler_params=pltpu.CompilerParams(
-            collective_id=0, has_side_effects=True, vmem_limit_bytes=63 << 20
+            collective_id=0, has_side_effects=True, vmem_limit_bytes=56<<20
         ),
         name="exchange",
     )(*scalars, *tensors, *nodes)
@@ -575,12 +573,8 @@
     def store(k):
         for i in range(8):
             rows = slice(i * BLK, (i + 1) * BLK)
-            pair_out[k, i] = (
-                pair[k, i].astype(F32) + gate[k, i].astype(F32) * both[k, rows, :CZ]
-            ).astype(BF16)
-            pair_grad[k, i] = (
-                both[k, rows, CZ:] - normed[k, rows, :].astype(F32) * along[k, rows, :]
-            ).astype(BF16)
+            pair_out[k, i] = pair[k, i] + gate[k, i] * both[k, rows, :CZ].astype(BF16)
+            pair_grad[k, i] = both[k, rows, CZ:].astype(BF16) - normed[k, rows, :] * along[k, rows, :].astype(BF16)
 
     norm(0)
     for k in range(STEP):
@@ -611,7 +605,7 @@
             pltpu.VMEM((STEP, 8 * BLK, 2 * CZ), F32),
             pltpu.VMEM((STEP, 8 * BLK, CZ), F32),
         ],
-        compiler_params=pltpu.CompilerParams(vmem_limit_bytes=62 << 20),
+        compiler_params=pltpu.CompilerParams(vmem_limit_bytes=42<<20),
         name="finish",
     )(pair, tri, grads, normed, gate, scale, out_w, bias_w)
 

time: 175 us -> 177 us (1.011)
  local copies, waits for them, and re-layouts: 0.63 us -> 4.54 us
    unnamed x3 -> x15, local copies, waits for them, and re-layouts: 0.63 us -> 4.54 us
    pallas_call x1, Pallas kernels: 19.9 us -> 17.8 us  [finish(): pl.pallas_call(finish_kernel, grid=(NB // STEP,), in_specs=[by_block(a) f...]
where the time goes in v5:
time: 177 us
  Pallas kernels  172 us (97%)
  local copies, waits for them, and re-layouts  4.54 us (3%)
    pallas_call x1, Pallas kernels, exchange(): pl.pallas_call(exchange_kernel, in_specs=[smem] * 4 + [anyspace] + [vmem]...  154 us
    pallas_call x1, Pallas kernels, finish(): pl.pallas_call(finish_kernel, grid=(NB // STEP,), in_specs=[by_block(a) f...  17.8 us
    unnamed x15, local copies, waits for them, and re-layouts  4.54 us

profile of v5, /device:TPU:1, one launch (start us, length us, event | category | flops | bytes accessed | tf_op | source)
XLA Modules:
  0.0 176.9 jit_solution(18341405820644022428)
XLA Ops:
  0.6 0.0 copy-start.5
  0.6 0.0 copy-start.4
  0.7 0.0 copy-start
  0.7 153.8 %exchange.1 = (bf16[24,4,16,8,128]{4,3,2,1,0:T(8,128)(2,1)}, bf16[24,16,8,128]{3,2,1,0:T(8,128)(2,1)}, bf16[32,768]{1,0:T(8,128)(2,1)}, bf16[24,1024,128]{2,1,0:...) custom-call(s32[6,32]{1,0:T(8,128)} %bitcast.18, s32[6,32]{1,0:T(8,128)} %bitcast.19, s32[32]{0:T(128)} %refs_2_.1, ...), custom_call_target="tpu_custom_call" | custom-call | tf_op jit(solution)/shard_map/exchange/pallas_call | solution.py:523
  154.5 0.0 copy-done.5
  154.5 0.0 copy-done.4
  154.5 0.0 copy-done
  154.5 0.0 copy-start.1
  154.5 1.9 %copy-done.1 = bf16[24,4,16,8,128]{4,3,2,1,0:T(8,128)(2,1)S(1)} copy-done((bf16[24,4,16,8,128]{4,3,2,1,0:T(8,128)(2,1)S(1)}, bf16[24,4,16,8,128]{4,3,2,1,0:T(8,128)(2,1)}, u32[]{:S(2)}) %copy-start.1) | copy-done | bytes 3145752
  156.4 0.0 copy-start.2
  156.4 1.1 copy-done.2
  157.5 0.0 copy-start.3
  157.5 0.9 copy-done.3
  158.4 0.0 copy-start.6
  158.4 17.8 %finish.1 = (bf16[24,8,128,128]{3,2,1,0:T(8,128)(2,1)}, bf16[24,8,128,128]{3,2,1,0:T(8,128)(2,1)}) custom-call(bf16[24,8,128,128]{3,2,1,0:T(8,128)(2,1)S(1)} %bitcast.11, bf16[24,64,8,128]{3,2,1,0:T(8,128)(2,1)S(1)} %bitcast.12, bf16[24,16,8,128]{3,2,1,0:T(8,128)(2,1)S(1)} %copy-done.2, bf16[24,1024,128]{2,1,0:T(8,128)(2,1)} %get-tuple-element.13.normed, ...), custom_call_target="tpu_custom_call" | custom-call | tf_op jit(solution)/shard_map/finish/pallas_call | solution.py:594
  176.3 0.0 copy-done.6
  176.3 0.6 copy.19
Async XLA Ops:
  0.6 153.8 %copy-start.5 = (bf16[128,16]{0,1:T(8,128)(2,1)S(1)}, bf16[128,16]{0,1:T(8,128)(2,1)}, u32[]{:S(2)}) copy-start(bf16[128,16]{0,1:T(8,128)(2,1)} %param.25) | copy-start | bytes 12292
  0.6 153.8 %copy-start.4 = (bf16[64,128]{1,0:T(8,128)(2,1)S(1)}, bf16[64,128]{1,0:T(8,128)(2,1)}, u32[]{:S(2)}) copy-start(bf16[64,128]{1,0:T(8,128)(2,1)} %out_w.1) | copy-start | bytes 49156
  0.7 153.8 %copy-start = (bf16[4,6,8,128,128]{4,3,2,1,0:T(8,128)(2,1)S(1)}, bf16[4,6,8,128,128]{4,3,2,1,0:T(8,128)(2,1)}, u32[]{:S(2)}) copy-start(bf16[4,6,8,128,128]{4,3,2,1,0:T(8,128)(2,1)} %param.15) | copy-start | bytes 18874372
  154.5 1.9 %copy-start.1 = (bf16[24,4,16,8,128]{4,3,2,1,0:T(8,128)(2,1)S(1)}, bf16[24,4,16,8,128]{4,3,2,1,0:T(8,128)(2,1)}, u32[]{:S(2)}) copy-start(bf16[24,4,16,8,128]{4,3,2,1,0:T(8,128)(2,1)} %get-tuple-element.11) | copy-start | bytes 9437188
  156.4 1.1 copy-start.2
  157.5 0.9 copy-start.3
  158.4 17.8 %copy-start.6 = (bf16[32,768]{1,0:T(8,128)(2,1)S(1)}, bf16[32,768]{1,0:T(8,128)(2,1)}, u32[]{:S(2)}) copy-start(bf16[32,768]{1,0:T(8,128)(2,1)} %get-tuple-element.23) | copy-start | bytes 147460

commit v6 on v5

--- a/solution.py
+++ b/solution.py
@@ -534,7 +534,7 @@
         ],
         scratch_shapes=scratch,
         compiler_params=pltpu.CompilerParams(
-            collective_id=0, has_side_effects=True, vmem_limit_bytes=56<<20
+            collective_id=0, has_side_effects=True, vmem_limit_bytes=63<<20
         ),
         name="exchange",
     )(*scalars, *tensors, *nodes)
@@ -605,7 +605,7 @@
             pltpu.VMEM((STEP, 8 * BLK, 2 * CZ), F32),
             pltpu.VMEM((STEP, 8 * BLK, CZ), F32),
         ],
-        compiler_params=pltpu.CompilerParams(vmem_limit_bytes=42<<20),
+        compiler_params=pltpu.CompilerParams(vmem_limit_bytes=62<<20),
         name="finish",
     )(pair, tri, grads, normed, gate, scale, out_w, bias_w)
 

time: 177 us -> 175 us (0.989)
  local copies, waits for them, and re-layouts: 4.54 us -> 0.63 us
    unnamed x15 -> x3, local copies, waits for them, and re-layouts: 4.54 us -> 0.63 us
    pallas_call x1, Pallas kernels: 17.8 us -> 19.9 us  [finish(): pl.pallas_call(finish_kernel, grid=(NB // STEP,), in_specs=[by_block(a) f...]
where the time goes in v6:
time: 175 us
  Pallas kernels  173 us (99%)
    pallas_call x1, Pallas kernels, exchange(): pl.pallas_call(exchange_kernel, in_specs=[smem] * 4 + [anyspace] + [vmem]...  153 us
    pallas_call x1, Pallas kernels, finish(): pl.pallas_call(finish_kernel, grid=(NB // STEP,), in_specs=[by_block(a) f...  19.9 us

profile of v6, /device:TPU:1, one launch (start us, length us, event | category | flops | bytes accessed | tf_op | source)
XLA Modules:
  0.0 174.6 jit_solution(12168391963738996399)
XLA Ops:
  0.6 153.4 %exchange.1 = (bf16[24,4,16,8,128]{4,3,2,1,0:T(8,128)(2,1)}, bf16[24,16,8,128]{3,2,1,0:T(8,128)(2,1)}, bf16[32,768]{1,0:T(8,128)(2,1)}, bf16[24,1024,128]{2,1,0:...) custom-call(s32[6,32]{1,0:T(8,128)} %bitcast.18, s32[6,32]{1,0:T(8,128)} %bitcast.19, s32[32]{0:T(128)} %refs_2_.1, ...), custom_call_target="tpu_custom_call" | custom-call | tf_op jit(solution)/shard_map/exchange/pallas_call | solution.py:523
  154.0 0.0 copy-start
  154.0 19.9 %finish.1 = (bf16[24,8,128,128]{3,2,1,0:T(8,128)(2,1)}, bf16[24,8,128,128]{3,2,1,0:T(8,128)(2,1)}) custom-call(bf16[24,8,128,128]{3,2,1,0:T(8,128)(2,1)} %bitcast.11, bf16[24,64,8,128]{3,2,1,0:T(8,128)(2,1)} %bitcast.12, bf16[24,16,8,128]{3,2,1,0:T(8,128)(2,1)} %get-tuple-element.12.grads, bf16[24,1024,128]{2,1,0:T(8,128)(2,1)} %get-tuple-element.13.normed, ...), custom_call_target="tpu_custom_call" | custom-call | tf_op jit(solution)/shard_map/finish/pallas_call | solution.py:594
  173.9 0.0 copy-done
  173.9 0.6 copy.19
Async XLA Ops:
  154.0 19.9 %copy-start = (bf16[32,768]{1,0:T(8,128)(2,1)S(1)}, bf16[32,768]{1,0:T(8,128)(2,1)}, u32[]{:S(2)}) copy-start(bf16[32,768]{1,0:T(8,128)(2,1)} %get-tuple-element.23) | copy-start | bytes 147460
